TPU v7x, 32 devices: a whole 2x2x4 slice. The times are simulated.
32 devices in a mesh: patch: 4 (over z), seg: 8 (over y, x, core).
Axes of the slice: x: 2, y: 2, z: 4, core: 2. Of those that a mesh axis runs over, the one named last changes fastest.
Arguments:
- slave_local: int32 [65536], P(('patch', 'seg')), may hold values from 0 to 511
- owner_route: int32 [65536, 1], P(('patch', 'seg')), may hold values from 0 to 31; in each aligned block of 2048 rows (0 to 2047, 2048 to 4095, ...) at most 128 rows name the same one
- master_local: int32 [65536], P(('patch', 'seg')), may hold values from 0 to 511
- quad_slave: float32 [65536, 2, 128], P(('patch', 'seg')), may hold values from -1 to 1
- quad_master: float32 [65536, 2, 128], P(('patch', 'seg')), may hold values from -1 to 1
- quad_weight: float32 [65536, 128], P(('patch', 'seg')), may hold values from 0.01 to 0.1
- slave_coords: float32 [3, 9, 16384], P(None, None, ('patch', 'seg')), may hold values from -6 to 6
- slave_disp: float32 [3, 9, 16384], P(None, None, ('patch', 'seg')), may hold values from -4 to 4
- slave_normals: float32 [3, 9, 16384], P(None, None, ('patch', 'seg')), may hold values from -6 to 6
- multipliers: float32 [3, 9, 16384], P(None, None, ('patch', 'seg')), may hold values from -6 to 6
- master_coords: float32 [3, 9, 16384], P(None, None, ('patch', 'seg')), may hold values from -6 to 6
- master_disp: float32 [3, 9, 16384], P(None, None, ('patch', 'seg')), may hold values from -4 to 4
Outputs:
- coupling: float32 [81, 65536], P(None, ('patch', 'seg'))
- weighted_gap: float32 [9, 16384], P(None, ('patch', 'seg'))
- slave_mass: float32 [81, 16384], P(None, ('patch', 'seg'))
- master_force: float32 [27, 16384], P(None, ('patch', 'seg'))
- master_mass: float32 [81, 16384], P(None, ('patch', 'seg'))
Inputs may be any that keep to these rules, and one draw needn't show every extreme that they name: `owner_route`: among the pairs of one device, no owner is named by more than 128 pairs, a bound that some block reaches.
All inputs are finite; a program needn't handle non-finite values.
Results may differ from a plain program's by a relative error of at most 0.0003.
Values sent between devices are 32-bit elements; how exact they have to be, the bound alone decides.
No kernel may reach another device: no remote copies, remote signals or barrier semaphores. Data moves between devices by JAX's collectives and lax.ppermute only.
A program may use at most 256 MiB of HBM per device.

v0:
```python
import jax
import jax.numpy as jnp
from jax import lax
from jax.sharding import PartitionSpec as P


def lagrange_rows(t):
    return jnp.stack([0.5 * t * (t - 1.0), 1.0 - t * t, 0.5 * t * (t + 1.0)], axis=1)


def shape_values(points):
    first = lagrange_rows(points[:, 0, :])
    second = lagrange_rows(points[:, 1, :])
    product = second[:, :, None, :] * first[:, None, :, :]
    return product.reshape(points.shape[0], 9, points.shape[2])


def shards(
    slave_local,
    owner_route,
    master_local,
    quad_slave,
    quad_master,
    quad_weight,
    slave_coords,
    slave_disp,
    slave_normals,
    multipliers,
    master_coords,
    master_disp,
):
    highest = lax.Precision.HIGHEST
    pairs = slave_local.shape[0]
    segments = slave_coords.shape[2]
    devices = lax.axis_size(("patch", "seg"))
    cap = 2 * pairs // devices
    owners = owner_route[:, 0]
    order = jnp.argsort(owners, stable=True)
    sorted_owner = owners[order]
    counts = jnp.sum(
        (owners[:, None] == jnp.arange(devices, dtype=jnp.int32)[None, :]).astype(jnp.int32), axis=0
    )
    starts = jnp.cumsum(counts) - counts
    ranks = jnp.arange(pairs, dtype=jnp.int32) - starts[sorted_owner]
    slots = jnp.zeros((pairs,), jnp.int32).at[order].set(sorted_owner * cap + ranks)
    request = jnp.full((devices * cap,), -1, jnp.int32).at[slots].set(master_local)
    asked = lax.all_to_all(request, ("patch", "seg"), split_axis=0, concat_axis=0, tiled=True)
    rows_owned = jnp.clip(asked, 0, segments - 1)
    table = (master_coords + master_disp).reshape(27, segments)
    reply = jnp.take(table, rows_owned, axis=1)
    arrived = lax.all_to_all(reply, ("patch", "seg"), split_axis=1, concat_axis=1, tiled=True)
    master_pos = jnp.take(arrived, slots, axis=1).reshape(3, 9, pairs)
    slave_shape = shape_values(quad_slave)
    master_shape = shape_values(quad_master)
    weighted = slave_shape * quad_weight[:, None, :]
    block_coupling = jnp.einsum("paq,pbq->abp", weighted, master_shape, precision=highest)
    slave_pos = jnp.take(slave_coords + slave_disp, slave_local, axis=2)
    normals = jnp.take(slave_normals, slave_local, axis=2)
    lam = jnp.take(multipliers, slave_local, axis=2)
    slave_points = jnp.einsum("kap,paq->kpq", slave_pos, slave_shape, precision=highest)
    master_points = jnp.einsum("kap,paq->kpq", master_pos, master_shape, precision=highest)
    normal_points = jnp.einsum("kap,paq->kpq", normals, slave_shape, precision=highest)
    gap = jnp.sum(normal_points * (master_points - slave_points), axis=0)
    gap_terms = jnp.einsum("paq,pq->ap", weighted, gap, precision=highest)
    mass_terms = jnp.einsum("paq,pcq->acp", weighted, slave_shape, precision=highest).reshape(
        81, pairs
    )
    force_terms = jnp.einsum("abp,kap->kbp", block_coupling, lam, precision=highest).reshape(
        27, pairs
    )
    master_weighted = master_shape * quad_weight[:, None, :]
    master_terms = jnp.einsum(
        "pbq,pcq->bcp", master_weighted, master_shape, precision=highest
    ).reshape(81, pairs)
    weighted_gap = jax.ops.segment_sum(gap_terms.T, slave_local, num_segments=segments).T
    slave_mass = jax.ops.segment_sum(mass_terms.T, slave_local, num_segments=segments).T
    outgoing_terms = jnp.concatenate([force_terms, master_terms], axis=0)
    rows_sent = outgoing_terms.shape[0]
    outgoing = jnp.zeros((rows_sent, devices * cap), jnp.float32).at[:, slots].set(outgoing_terms)
    incoming = lax.all_to_all(outgoing, ("patch", "seg"), split_axis=1, concat_axis=1, tiled=True)
    totals = jax.ops.segment_sum(incoming.T, rows_owned, num_segments=segments).T
    master_mass = totals[27:]
    coupling = block_coupling.reshape(81, pairs)
    return (coupling, weighted_gap, slave_mass, totals[:27], master_mass)


def solution(mesh):
    return jax.shard_map(
        shards,
        mesh=mesh,
        in_specs=(
            P(("patch", "seg")),
            P(("patch", "seg"), None),
            P(("patch", "seg")),
            P(("patch", "seg"), None, None),
            P(("patch", "seg"), None, None),
            P(("patch", "seg"), None),
            P(None, None, ("patch", "seg")),
            P(None, None, ("patch", "seg")),
            P(None, None, ("patch", "seg")),
            P(None, None, ("patch", "seg")),
            P(None, None, ("patch", "seg")),
            P(None, None, ("patch", "seg")),
        ),
        out_specs=(
            P(None, ("patch", "seg")),
            P(None, ("patch", "seg")),
            P(None, ("patch", "seg")),
            P(None, ("patch", "seg")),
            P(None, ("patch", "seg")),
        ),
        check_vma=False,
    )
```

profile of v0, /device:TPU:0, one launch (start us, length us, event | category | flops | bytes accessed | tf_op | source)
XLA Modules:
  0.0 600.6 jit_solution(3236960536532887433)
XLA Ops:
  3.3 5.7 sort.17
  9.0 11.8 %gather_fusion = s32[2048]{0:T(1024)S(1)} fusion(s32[2048]{0:T(1024)S(1)} %bitcast.96, s32[2048]{0:T(1024)S(1)} %get-tuple-element.81), kind=kCustom, calls=%fused_computation.3 | custom fusion | bytes 24576 | tf_op jit(solution)/shard_map/gather | solution.py:39
  20.8 4.3 compare_select_fusion.3
  25.8 15.7 %fusion.58 = s32[2048]{0:T(1024)S(1)} fusion(pred[2048]{0:T(1024)(128)(4,1)S(1)} %get-tuple-element.62, pred[2048]{0:T(1024)(128)(4,1)S(1)} %get-tuple-element.61, pred[2048]{0:T(1024)(128)(4,1)S(1)} %get-tuple-element.60, pred[2048]{0:T(1024)(128)(4,1)S(1)} %get-tuple-element.59, pred[2048]{0:T(1024)(128)(4,1)S(1)} %get-tuple-element.58, ...), kind=kLoop, calls=%fused_computation.120 | loop fusion | flops 57344 | bytes 75876 | tf_op jit(solution)/shard_map/add | solution.py:45
  41.5 8.0 %scatter_custom_fusion = s32[2048]{0:T(1024)S(1)} fusion(s32[2048]{0:T(1024)S(1)} %get-tuple-element.82, s32[2048]{0:T(1024)S(1)} %fusion.58, s32[]{:T(128)} %constant.33.clone.1), kind=kCustom, calls=%fused_computation.129 | custom fusion | bytes 8196 | tf_op jit(solution)/shard_map/scatter | solution.py:45
  50.2 8.8 %scatter_custom_fusion.1 = s32[4096]{0:T(1024)} fusion(s32[2048]{0:T(1024)S(1)} %get-tuple-element.80, s32[2048]{0:T(1024)} %param.16, s32[]{:T(128)} %constant.45.clone.1), kind=kCustom, calls=%fused_computation.122 | custom fusion | bytes 16896 | tf_op jit(solution)/shard_map/scatter | solution.py:46
  59.0 7.6 %all-to-all-start = ((s32[32,128,1]{1,2,0:T(1,128)}), s32[32,128,1]{1,2,0:T(1,128)}, u32[]{:S(2)}, u32[]{:S(2)}) async-start(s32[32,128,1]{1,2,0:T(1,128)} %bitcast.40), calls=%async_computation | async-start | bytes 32768 | tf_op jit(solution)/shard_map/all_to_all | solution.py:47
  67.1 4.6 add_multiply_fusion.3
  71.7 5.8 pad_maximum_fusion.2
  77.9 1.4 copy-done.5
  79.3 4.6 add_multiply_fusion.7
  83.8 5.8 pad_maximum_fusion
  89.6 1.8 copy.165
  91.5 1.8 copy.166
  94.0 10.6 %broadcast_multiply_fusion.3 = f32[2048,3,3,128]{3,0,2,1:T(8,128)} fusion(f32[2048,3,128]{2,0,1:T(8,128)} %copy.166, f32[2048,3,128]{2,0,1:T(8,128)} %copy.165), kind=kLoop, calls=%fused_computation.35 | loop fusion | flops 2359296 | bytes 15728640 | tf_op jit(solution)/shard_map/mul | solution.py:14
  104.6 9.6 %broadcast_multiply_fusion = (f32[2048,9,128]{2,0,1:T(8,128)}, f32[2048,9,128]{2,0,1:T(8,128)}) fusion(f32[2048,128]{1,0:T(8,128)S(1)} %copy-done.6, f32[2048,3,3,128]{3,0,2,1:T(8,128)} %broadcast_multiply_fusion.3, f32[2048,3,3,128]{3,0,2,1:T(8,128)S(1)} %broadcast_multiply_fusion.2), kind=kLoop, calls=%fused_computation.32 | loop fusion | flops 4718592 | bytes 38797312 | tf_op jit(solution)/shard_map/mul | solution.py:71
  114.2 41.5 %fusion.17 = f32[9,9,2048]{0,1,2:T(8,128)} fusion(f32[2048,9,128]{2,0,1:T(8,128)} %get-tuple-element.77, f32[2048,9,128]{2,0,1:T(8,128)} %bitcast.102), kind=kOutput, calls=%fused_computation.29 | convolution fusion | flops 254803968 | bytes 19537920 | tf_op jit(solution)/shard_map/pbq,pcq->bcp/dot_general | solution.py:72
  155.7 10.0 %copy.193 = f32[9,9,2048]{2,1,0:T(8,128)S(1)} copy(f32[9,9,2048]{0,1,2:T(8,128)} %fusion.17) | data formatting | bytes 1327104 | tf_op jit(solution)/shard_map/pbq,pcq->bcp/transpose | solution.py:72
  165.8 0.9 reshape.147
  166.7 41.9 %fusion.22 = f32[9,9,2048]{0,1,2:T(8,128)} fusion(f32[2048,9,128]{2,0,1:T(8,128)} %get-tuple-element.78, f32[2048,9,128]{2,0,1:T(8,128)} %bitcast.103), kind=kOutput, calls=%fused_computation.30 | convolution fusion | flops 254803968 | bytes 19537920 | tf_op jit(solution)/shard_map/paq,pbq->abp/dot_general | solution.py:56
  208.6 49.3 %fusion.27 = f32[9,9,2048]{0,1,2:T(8,128)} fusion(f32[2048,9,128]{2,0,1:T(8,128)} %get-tuple-element.78, f32[2048,9,128]{2,0,1:T(8,128)S(1)} %bitcast.101), kind=kOutput, calls=%fused_computation.31 | convolution fusion | flops 254803968 | bytes 19537920 | tf_op jit(solution)/shard_map/paq,pcq->acp/dot_general | solution.py:65
  257.9 15.3 %gather_fusion.5 = f32[2048,3,9]{2,1,0:T(4,128)} fusion(f32[3,9,512]{1,0,2:T(4,128)S(1)} %copy.188, s32[2048]{0:T(1024)S(1)} %fusion.61), kind=kCustom, calls=%fused_computation.2.clone | custom fusion | bytes 450560 | tf_op jit(solution)/shard_map/jit(_take)/gather | solution.py:59
  273.2 33.2 %fusion.39 = f32[3,9,2048]{1,0,2:T(4,128)} fusion(f32[9,9,2048]{0,1,2:T(8,128)} %fusion.22, f32[2048,3,9]{2,1,0:T(4,128)} %gather_fusion.5, pred[2048]{0:T(1024)(128)(4,1)S(1)} %compare_and_fusion.1), kind=kOutput, calls=%fused_computation.48 | convolution fusion | flops 6027264 | bytes 1107968 | tf_op jit(solution)/shard_map/abp,kap->kbp/dot_general | solution.py:68
  306.4 3.4 copy.190
  310.0 10.1 %copy.171 = f32[9,9,2048]{2,1,0:T(8,128)S(1)} copy(f32[9,9,2048]{0,1,2:T(8,128)} %fusion.22) | data formatting | bytes 1327104 | tf_op jit(solution)/shard_map/paq,pbq->abp/transpose | solution.py:56
  320.8 2.2 copy.172
  323.1 16.6 %gather_fusion.3 = f32[2048,3,9]{2,1,0:T(4,128)} fusion(f32[3,9,512]{1,0,2:T(4,128)} %copy.172, s32[2048]{0:T(1024)S(1)} %fusion.61), kind=kCustom, calls=%fused_computation.clone | custom fusion | bytes 450560 | tf_op jit(solution)/shard_map/jit(_take)/gather | solution.py:58
  339.6 15.4 %gather_fusion.4 = f32[2048,3,9]{2,1,0:T(4,128)} fusion(f32[3,9,512]{1,0,2:T(4,128)S(1)} %copy.182, s32[2048]{0:T(1024)S(1)} %fusion.61), kind=kCustom, calls=%fused_computation.1.clone | custom fusion | bytes 450560 | tf_op jit(solution)/shard_map/jit(_take)/gather | solution.py:57
  355.0 10.0 %copy.186 = f32[9,9,2048]{2,1,0:T(8,128)S(1)} copy(f32[9,9,2048]{0,1,2:T(8,128)} %fusion.27) | data formatting | bytes 1327104 | tf_op jit(solution)/shard_map/paq,pcq->acp/transpose | solution.py:65
  365.1 1.0 reshape.145
  367.0 1.4 copy.194
  368.7 12.1 %scatter_custom_fusion.3 = f32[512,81]{1,0:T(8,128)S(1)} fusion(s32[2048]{0:T(1024)} %param.14, f32[2048,81]{1,0:T(8,128)S(1)} %copy.187, f32[]{:T(128)} %constant.32.clone.1), kind=kCustom, calls=%fused_computation.76 | custom fusion | flops 165888 | bytes 166400 | tf_op jit(solution)/shard_map/scatter-add | solution.py:76
  381.7 6.5 %scatter_custom_fusion.4 = f32[108,4096]{0,1:T(8,128)S(1)} fusion(s32[2048]{0:T(1024)} %copy-done.16, f32[2048,108]{1,0:T(8,128)} %copy.194, f32[]{:T(128)} %constant.32.clone.1), kind=kCustom, calls=%fused_computation.55 | custom fusion | bytes 1769984 | tf_op jit(solution)/shard_map/scatter | solution.py:79
  388.1 1.9 copy.195
  391.5 10.8 %gather_fusion.1 = f32[4096,27]{1,0:T(8,128)S(1)} fusion(f32[27,512]{0,1:T(8,128)S(1)} %copy.176, s32[4096]{0:T(1024)S(1)} %broadcast_clamp_fusion), kind=kCustom, calls=%fused_computation.4 | custom fusion | bytes 901120 | tf_op jit(solution)/shard_map/jit(_take)/gather | solution.py:50
  403.8 6.0 all-to-all-start.1
  409.8 28.4 %fusion.4 = f32[2048,128,3]{1,2,0:T(4,128)} fusion(f32[2048,9,128]{2,0,1:T(8,128)} %bitcast.97, f32[2048,3,9]{2,1,0:T(4,128)} %gather_fusion.3, pred[2048]{0:T(1024)(128)(4,1)S(1)} %compare_and_fusion.1), kind=kOutput, calls=%fused_computation.16 | convolution fusion | flops 84989952 | bytes 12806144 | tf_op jit(solution)/shard_map/kap,paq->kpq/dot_general | solution.py:62
  438.2 6.1 %all-to-all-start.2 = ((f32[108,32,128]{2,0,1:T(8,128)}), f32[108,32,128]{2,0,1:T(8,128)}, u32[]{:S(2)}, u32[]{:S(2)}) async-start(f32[108,32,128]{2,0,1:T(8,128)} %copy.195), calls=%async_computation.2 | async-start | bytes 3670016 | tf_op jit(solution)/shard_map/all_to_all | solution.py:80
  444.4 28.4 %fusion.2 = f32[2048,128,3]{1,2,0:T(4,128)} fusion(f32[2048,9,128]{2,0,1:T(8,128)} %bitcast.98, f32[2048,3,9]{2,1,0:T(4,128)} %gather_fusion.4, pred[2048]{0:T(1024)(128)(4,1)S(1)} %compare_and_fusion.1), kind=kOutput, calls=%fused_computation.14 | convolution fusion | flops 84989952 | bytes 12806144 | tf_op jit(solution)/shard_map/kap,paq->kpq/dot_general | solution.py:60
  473.4 5.5 gather_fusion.2
  479.3 3.2 copy.181
  482.5 32.1 %multiply_reduce_fusion = f32[2048,128]{1,0:T(8,128)S(1)} fusion(f32[2048,128,3]{1,2,0:T(4,128)} %fusion.4, f32[2048,128,3]{1,2,0:T(4,128)} %fusion.2, f32[3,9,2048]{1,0,2:T(4,128)} %copy.181, f32[2048,9,128]{2,0,1:T(8,128)} %bitcast.104), kind=kOutput, calls=%fused_computation.47 | convolution fusion | flops 87031808 | bytes 16998400 | tf_op jit(solution)/shard_map/kap,paq->kpq/dot_general | solution.py:61
  514.6 39.8 %fusion.7 = f32[2048,1,9]{2,1,0:T(1,128)S(1)} fusion(f32[2048,128,1]{1,2,0:T(1,128)S(1)} %bitcast.111, f32[2048,9,128]{2,0,1:T(8,128)S(1)} %bitcast.106), kind=kOutput, calls=%fused_computation.19 | convolution fusion | flops 28311552 | bytes 10559488 | tf_op jit(solution)/shard_map/paq,pq->ap/dot_general | solution.py:64
  554.4 11.7 %scatter_custom_fusion.2 = f32[512,9]{1,0:T(8,128)S(1)} fusion(s32[2048]{0:T(1024)} %param.14, f32[2048,9]{1,0:T(8,128)S(1)} %bitcast.116, f32[]{:T(128)} %constant.32.clone.1), kind=kCustom, calls=%fused_computation.78 | custom fusion | flops 18432 | bytes 18944 | tf_op jit(solution)/shard_map/scatter-add | solution.py:75
  566.8 2.1 copy.196
  569.0 1.4 copy.205
  570.4 1.9 copy.197
  572.3 26.4 %scatter_custom_fusion.5 = f32[512,108]{1,0:T(8,128)S(1)} fusion(s32[4096]{0:T(1024)S(1)} %bitcast.122, f32[4096,108]{1,0:T(8,128)} %copy.197, f32[]{:T(128)} %constant.32.clone.1), kind=kCustom, calls=%fused_computation.74 | custom fusion | flops 442368 | bytes 221696 | tf_op jit(solution)/shard_map/scatter-add | solution.py:81
  (94 shorter events, 15.0 us)
Async XLA Ops:
  0.6 8.4 %copy-start = (s32[2048,1]{0,1:T(1,128)S(1)}, s32[2048,1]{0,1:T(1,128)}, u32[]{:S(2)}) copy-start(s32[2048,1]{0,1:T(1,128)} %param.15) | copy-start | bytes 24580
  9.0 57.6 %copy-start.15 = (s32[2048]{0:T(1024)S(1)}, s32[2048]{0:T(1024)}, u32[]{:S(2)}) copy-start(s32[2048]{0:T(1024)} %param.14) | copy-start | bytes 24580
  9.0 57.6 %copy-start.7 = (f32[3,9,512]{2,0,1:T(4,128)S(1)}, f32[3,9,512]{2,0,1:T(4,128)}, u32[]{:S(2)}) copy-start(f32[3,9,512]{2,0,1:T(4,128)} %param.23) | copy-start | bytes 165892
  9.0 58.0 %copy-start.4 = (f32[2048,2,128]{2,1,0:T(2,128)S(1)}, f32[2048,2,128]{2,1,0:T(2,128)}, u32[]{:S(2)}) copy-start(f32[2048,2,128]{2,1,0:T(2,128)} %param.17) | copy-start | bytes 6291460
  49.6 22.1 %copy-start.12 = (s32[2048]{0:T(1024)}, s32[2048]{0:T(1024)S(1)}, u32[]{:S(2)}) copy-start(s32[2048]{0:T(1024)S(1)} %scatter_custom_fusion) | copy-start | bytes 24580
  50.2 21.5 %copy-start.16 = (s32[2048]{0:T(1024)}, s32[2048]{0:T(1024)S(1)}, u32[]{:S(2)}) copy-start(s32[2048]{0:T(1024)S(1)} %get-tuple-element.80) | copy-start | bytes 24580
  59.0 331.0 %all-to-all-start = ((s32[32,128,1]{1,2,0:T(1,128)}), s32[32,128,1]{1,2,0:T(1,128)}, u32[]{:S(2)}, u32[]{:S(2)}) async-start(s32[32,128,1]{1,2,0:T(1,128)} %bitcast.40), calls=%async_computation | async-start | bytes 32768 | tf_op jit(solution)/shard_map/all_to_all | solution.py:47
  77.7 1.6 copy-start.5
  94.0 10.6 %copy-start.1 = (f32[2048,3,3,128]{3,0,2,1:T(8,128)}, f32[2048,3,3,128]{3,0,2,1:T(8,128)S(1)}, u32[]{:S(2)}) copy-start(f32[2048,3,3,128]{3,0,2,1:T(8,128)S(1)} %broadcast_multiply_fusion.2) | copy-start | bytes 28311556
  94.0 10.6 %copy-start.6 = (f32[2048,128]{1,0:T(8,128)S(1)}, f32[2048,128]{1,0:T(8,128)}, u32[]{:S(2)}) copy-start(f32[2048,128]{1,0:T(8,128)} %param.19) | copy-start | bytes 3145732
  165.8 42.8 %slice-start = ((s8[9437184]{0:T(1024)(128)(4,1)}), s8[1048576]{0:T(1024)(128)(4,1)S(1)}, s32[]{:S(2)}) async-start(s8[9437184]{0:T(1024)(128)(4,1)} %bitcast.99), calls=%async_computation.3 | async-start | bytes 2097152
  166.7 41.9 %slice-start.1 = ((s8[9437184]{0:T(1024)(128)(4,1)}), s8[4194304]{0:T(1024)(128)(4,1)S(1)}, s32[]{:S(2)}) async-start(s8[9437184]{0:T(1024)(128)(4,1)} %bitcast.99), calls=%async_computation.4 | async-start | bytes 8388608
  166.7 41.9 %slice-start.2 = ((s8[9437184]{0:T(1024)(128)(4,1)}), s8[4194304]{0:T(1024)(128)(4,1)S(1)}, s32[]{:S(2)}) async-start(s8[9437184]{0:T(1024)(128)(4,1)} %bitcast.99), calls=%async_computation.5 | async-start | bytes 8388608
  306.4 3.5 copy-start.3
  306.4 3.6 copy-start.13
  310.0 10.1 %copy-start.8 = (f32[3,9,512]{2,0,1:T(4,128)S(1)}, f32[3,9,512]{2,0,1:T(4,128)}, u32[]{:S(2)}) copy-start(f32[3,9,512]{2,0,1:T(4,128)} %param.24) | copy-start | bytes 165892
  310.0 10.1 %copy-start.9 = (f32[3,9,512]{2,0,1:T(4,128)S(1)}, f32[3,9,512]{2,0,1:T(4,128)}, u32[]{:S(2)}) copy-start(f32[3,9,512]{2,0,1:T(4,128)} %param.25) | copy-start | bytes 165892
  310.0 10.4 %copy-start.10 = (f32[3,9,512]{2,0,1:T(4,128)S(1)}, f32[3,9,512]{2,0,1:T(4,128)}, u32[]{:S(2)}) copy-start(f32[3,9,512]{2,0,1:T(4,128)} %param.20) | copy-start | bytes 165892
  310.0 10.4 %copy-start.11 = (f32[3,9,512]{2,0,1:T(4,128)S(1)}, f32[3,9,512]{2,0,1:T(4,128)}, u32[]{:S(2)}) copy-start(f32[3,9,512]{2,0,1:T(4,128)} %param.21) | copy-start | bytes 165892
  366.0 2.4 copy-start.2
  403.8 34.4 %all-to-all-start.1 = ((f32[27,32,128]{2,0,1:T(8,128)}), f32[27,32,128]{2,0,1:T(8,128)S(1)}, u32[]{:S(2)}, u32[]{:S(2)}) async-start(f32[27,32,128]{2,0,1:T(8,128)} %broadcast_select_fusion), calls=%async_computation.1 | async-start | bytes 1048576 | tf_op jit(solution)/shard_map/all_to_all | solution.py:51
  438.2 128.6 %all-to-all-start.2 = ((f32[108,32,128]{2,0,1:T(8,128)}), f32[108,32,128]{2,0,1:T(8,128)}, u32[]{:S(2)}, u32[]{:S(2)}) async-start(f32[108,32,128]{2,0,1:T(8,128)} %copy.195), calls=%async_computation.2 | async-start | bytes 3670016 | tf_op jit(solution)/shard_map/all_to_all | solution.py:80
  444.3 29.1 %copy-start.14 = (s32[2048]{0:T(1024)S(1)}, s32[2048]{0:T(1024)}, u32[]{:S(2)}) copy-start(s32[2048]{0:T(1024)} %get-tuple-element.79) | copy-start | bytes 24580
  479.3 35.3 %slice-start.3 = ((s8[9437184]{0:T(1024)(128)(4,1)}), s8[1048576]{0:T(1024)(128)(4,1)S(1)}, s32[]{:S(2)}) async-start(s8[9437184]{0:T(1024)(128)(4,1)} %bitcast.105), calls=%async_computation.6 | async-start | bytes 2097152
  482.5 32.1 %slice-start.4 = ((s8[9437184]{0:T(1024)(128)(4,1)}), s8[4194304]{0:T(1024)(128)(4,1)S(1)}, s32[]{:S(2)}) async-start(s8[9437184]{0:T(1024)(128)(4,1)} %bitcast.105), calls=%async_computation.7 | async-start | bytes 8388608
  482.5 32.1 %slice-start.5 = ((s8[9437184]{0:T(1024)(128)(4,1)}), s8[4194304]{0:T(1024)(128)(4,1)S(1)}, s32[]{:S(2)}) async-start(s8[9437184]{0:T(1024)(128)(4,1)} %bitcast.105), calls=%async_computation.8 | async-start | bytes 8388608
where the time goes:
time: 606 us; the launch traced here: 601 us
  matrix products  294 us (49%)
  local copies, waits for them, and re-layouts  162 us (27%)
  other arithmetic  122 us (20%)
  starting transfers between devices  19.7 us (3%)
    dot_general x1, matrix products, shards(): jnp.einsum('paq,pcq->acp', weighted, slave_shape, precision=highest)  49.3 us
    dot_general x1, matrix products, shards(): jnp.einsum('paq,pbq->abp', weighted, master_shape, precision=highest)  41.9 us
    dot_general x1, matrix products, shards(): jnp.einsum('pbq,pcq->bcp', master_weighted, master_shape, precision=highest)  41.5 us
    dot_general x1, matrix products, shards(): gap_terms = jnp.einsum('paq,pq->ap', weighted, gap, precision=highest)  39.8 us
    dot_general x1, matrix products, shards(): jnp.einsum('abp,kap->kbp', block_coupling, lam, precision=highest)  33.2 us
    dot_general x1, matrix products, shards(): jnp.einsum('kap,paq->kpq', master_pos, master_shape, precision=highest)  32.1 us
    dot_general x1, matrix products, shards(): jnp.einsum('kap,paq->kpq', slave_pos, slave_shape, precision=highest)  28.4 us
    dot_general x1, matrix products, shards(): jnp.einsum('kap,paq->kpq', normals, slave_shape, precision=highest)  28.4 us
  transfers between devices with their start and end apart: 3, of which 0 were waited for; matrix products, arithmetic and copies ran while one was open for 79% of the time, Pallas kernels for 0%

commit v1 on v0

v1 whole, which is shorter than its diff:
```python
import functools

import jax
import jax.numpy as jnp
import numpy as np
from jax import lax
from jax.experimental import pallas as pl
from jax.experimental.pallas import tpu as pltpu
from jax.sharding import PartitionSpec as P

AXES = ("patch", "seg")
BLOCK = 128
F32 = jnp.float32
BF16 = jnp.bfloat16


def axis_products():
    axis = np.zeros((3, 3, 5), np.float32)
    axis[0, 0] = (1, 0, 0, -0.75, 0.25)
    axis[0, 1] = axis[1, 0] = (0, 0, 0, 1, 0)
    axis[0, 2] = axis[2, 0] = (0, 0, 0, -0.25, -0.25)
    axis[1, 1] = (0, 1, 0, -1, -1)
    axis[1, 2] = axis[2, 1] = (0, 0, 0, 0, 1)
    axis[2, 2] = (0, 0, 1, 0.25, -0.75)
    return axis


def reduced(x, along):
    x = np.moveaxis(x, along, 0)
    x = np.concatenate([x[1:2], x[0:1] - x[1:2], x[2:3] - x[1:2], x[3:]], axis=0)
    return np.moveaxis(x, 0, along)


def extra_moments():
    return [(m, n) for m in (3, 4) for n in range(5)] + [(m, n) for m in range(3) for n in (3, 4)]


def expansion(plain):
    axis = axis_products()
    table = np.zeros((81, 32), np.float32)
    for b in range(9):
        for c in range(9):
            both = np.einsum("m,n->mn", axis[b % 3, c % 3], axis[b // 3, c // 3])
            mixed = reduced(reduced(both, 0), 1)
            base = both if plain else mixed
            for n in range(3):
                for m in range(3):
                    table[9 * b + c, 3 * n + m] = base[m, n]
            for at, (m, n) in enumerate(extra_moments()):
                table[9 * b + c, 9 + at] = mixed[m, n]
    return table


def basis(t):
    square = t * t
    low = 0.5 * (square - t)
    middle = 1.0 - square
    high = low + t
    return [low, middle, high, low * middle, middle * high]


def reduced_rows(x):
    def along(at, stride):
        out = [None] * 9
        for q in range(3):
            low, middle, high = (at[q * (4 - stride) + stride * i] for i in range(3))
            for i, block in enumerate((middle, low - middle, high - middle)):
                out[q * (4 - stride) + stride * i] = block
        return out

    return along(along(x, 1), 3)


def split2(x):
    high = x.astype(BF16)
    low = (x - high.astype(F32)).astype(BF16)
    return high, low


def stack2(x):
    high = x.astype(BF16).astype(F32)
    return jnp.concatenate([high, x - high], axis=0).astype(BF16)


def dot(a, b):
    return jnp.dot(a, b, preferred_element_type=F32)


def dot_nt(a, b):
    return lax.dot_general(a, b, (((1,), (1,)), ((), ())), preferred_element_type=F32)


def joined(product):
    half = product.shape[0] // 2
    return product[:half] + product[half:]


def one_hot(index_row, rows):
    at = lax.broadcasted_iota(jnp.int32, (rows, index_row.shape[1]), 0)
    return jnp.where(at == index_row, 1.0, 0.0).astype(BF16)


def total(x):
    return jnp.sum(x, axis=0, keepdims=True)


def planes(ref):
    return ref[pl.ds(0, BLOCK, stride=2), :].T, ref[pl.ds(1, BLOCK, stride=2), :].T


def product(*factors):
    value = None
    for x in factors:
        if x is not None:
            value = x if value is None else value * x
    return value


def extra_rows(w, first, second):
    first = [None, first[0], first[2], first[3], first[4]]
    second = [None, second[0], second[2], second[3], second[4]]
    weighted = [product(w, x) for x in first]
    return [total(product(weighted[m], second[n])) for m, n in extra_moments()]


def fill_rows(table_ref, start, blocks):
    half = table_ref.shape[0] // 2
    for a, block in enumerate(blocks):
        high, low = split2(block)
        at = start + 3 * a
        table_ref[at : at + 3, :] = high
        table_ref[at + half : at + half + 3, :] = low


def terms_kernel(qs_ref, qm_ref, w_ref, sl_ref, ml_ref, lam_ref, *rest):
    coupling_ref, terms_ref, planes_ref, shape_ref, c_ref, lam_table_ref = rest[-6:]
    segments = lam_ref.shape[2]

    @pl.when(pl.program_id(0) == 0)
    def _():
        fill_rows(lam_table_ref, 0, [lam_ref[a] for a in range(9)])

    w = w_ref[...].T
    s, t = planes(qs_ref)
    u, v = planes(qm_ref)
    for at, plane in enumerate((s, t, u, v, w)):
        planes_ref[at] = plane
    fs, ft, fu, fv = basis(s)[:3], basis(t)[:3], basis(u), basis(v)
    for b in range(9):
        shape_ref[b] = fu[b % 3] * fv[b // 3]
    base = None
    for a in range(9):
        weighted = (w * fs[a % 3]) * ft[a // 3]
        for b in range(9):
            c_ref[a, b : b + 1, :] = total(weighted * shape_ref[b])
    lam = joined(dot(lam_table_ref[...], one_hot(sl_ref[...], segments)))
    for k in range(3):
        force = c_ref[0, 0:9, :] * lam[k : k + 1, :]
        for a in range(1, 9):
            force = force + c_ref[a, 0:9, :] * lam[3 * a + k : 3 * a + k + 1, :]
        terms_ref[9 * k : 9 * k + 9, :] = force
    base = c_ref[0, 0:9, :]
    coupling_ref[0:9, :] = base
    for a in range(1, 9):
        block = c_ref[a, 0:9, :]
        coupling_ref[9 * a : 9 * a + 9, :] = block
        base = base + block
    terms_ref[27:36, :] = base
    for at, row in enumerate(extra_rows(w, fu, fv)):
        terms_ref[36 + at : 37 + at, :] = row
    terms_ref[52:53, :] = ml_ref[...].astype(F32)
    terms_ref[53:56, :] = jnp.zeros((3, BLOCK), F32)


def slots_kernel(owner_ref, terms_ref, out_ref, left_ref, *, devices, cap):
    pairs = owner_ref.shape[1]
    width = 256
    per = width // cap
    groups = devices // per
    owner = owner_ref[...]
    upper = jnp.where(
        lax.broadcasted_iota(jnp.int32, (width, width), 0) < lax.broadcasted_iota(jnp.int32, (width, width), 1),
        1.0,
        0.0,
    ).astype(BF16)
    carry = jnp.zeros((devices, 1), F32)
    ranks = []
    for at in range(0, pairs, width):
        mine = one_hot(owner[:, at : at + width], devices)
        before = dot(mine, upper) + carry
        wide = mine.astype(F32)
        ranks.append(total(wide * before))
        carry = carry + jnp.sum(wide, axis=1, keepdims=True)
    rank = jnp.concatenate(ranks, axis=1).astype(jnp.int32)
    group = owner // per
    column = (owner - group * per) * cap + rank
    place = one_hot(column, width)
    both = stack2(terms_ref[...])
    rows = both.shape[0]
    for g in range(groups):
        left_ref[g * rows : (g + 1) * rows, :] = both * jnp.where(group == g, 1.0, 0.0).astype(BF16)
    sent = dot_nt(left_ref[...], place)
    for g in range(groups):
        block = joined(sent[g * rows : (g + 1) * rows])
        if cap == 128:
            out_ref[2 * g] = block[:, :128]
            out_ref[2 * g + 1] = block[:, 128:]
        else:
            out_ref[g] = block


def table_kernel(coords_ref, disp_ref, out_ref, rows_ref):
    rows_ref[...] = jnp.zeros_like(rows_ref)
    for i, block in enumerate(reduced_rows([coords_ref[a] + disp_ref[a] for a in range(9)])):
        for c in range(block.shape[1] // 128):
            at = 32 * c + 3 * i
            rows_ref[at : at + 3, :] = block[:, 128 * c : 128 * (c + 1)]
    out_ref[...] = rows_ref[...].T


def gap_kernel(
    row_ref, planes_ref, sl_ref, ml_ref, coords_ref, disp_ref, normals_ref, expand_ref, near_ref, far_ref,
    gap_ref, mass_ref, table_ref, slave_ref, sums_ref, a_ref, picked_ref, sems,
):
    segments = coords_ref.shape[2]
    step = pl.program_id(0)

    @pl.when(step == 0)
    def _():
        half = near_ref.shape[0]
        copies = [
            pltpu.make_async_copy(near_ref, table_ref.at[pl.ds(0, half)], sems.at[0]),
            pltpu.make_async_copy(far_ref, table_ref.at[pl.ds(half, half)], sems.at[1]),
        ]
        for copy in copies:
            copy.start()
        sums_ref[...] = jnp.zeros_like(sums_ref)
        a_ref[...] = jnp.zeros_like(a_ref)
        slave_ref[...] = jnp.zeros_like(slave_ref)
        fill_rows(slave_ref, 0, reduced_rows([coords_ref[a] + disp_ref[a] for a in range(9)]))
        fill_rows(slave_ref, 32, reduced_rows([normals_ref[a] for a in range(9)]))
        for copy in copies:
            copy.wait()

    hot_slave = one_hot(sl_ref[...], segments)
    slave = joined(dot(slave_ref[...], hot_slave))
    for p in range(BLOCK):
        picked_ref[p : p + 1, :] = table_ref[pl.ds(row_ref[step * BLOCK + p], 1), :]
    picked = picked_ref[...].T
    quarter = ml_ref[...] // 128
    position = picked[0:32]
    for c in range(1, segments // 128):
        position = jnp.where(quarter == c, picked[32 * c : 32 * c + 32], position)

    s, t, u, v, w = (planes_ref[at] for at in range(5))
    fs, ft = basis(s), basis(t)
    fu, fv = basis(u), basis(v)

    def field(coefs, row, first, second):
        value = None
        for j in range(3):
            c = [coefs[row + 9 * j + 3 * i : row + 9 * j + 3 * i + 1] for i in range(3)]
            part = c[0] + c[1] * first[0] + c[2] * first[2]
            value = part if j == 0 else value + part * second[0 if j == 1 else 2]
        return value

    gap = None
    for k in range(3):
        normal = field(slave, 32 + k, fs, ft)
        away = field(position, k, fu, fv) - field(slave, k, fs, ft)
        gap = normal * away if gap is None else gap + normal * away
    for n in range(3):
        for m in range(3):
            a = 3 * n + m
            weighted = product(w, (None, fs[0], fs[2])[m], (None, ft[0], ft[2])[n])
            a_ref[a : a + 1, :] = total(weighted)
            a_ref[32 + a : 33 + a, :] = total(weighted * gap)
    for at, row in enumerate(extra_rows(w, fs, ft)):
        a_ref[9 + at : 10 + at, :] = row
    sums_ref[...] += joined(dot_nt(stack2(a_ref[...]), hot_slave))

    @pl.when(step == pl.num_programs(0) - 1)
    def _():
        for j in range(3):
            for i in range(3):
                row = None
                for m, n, sign in lagrange_terms(i, j):
                    part = sums_ref[32 + 3 * n + m : 33 + 3 * n + m, :] * sign
                    row = part if row is None else row + part
                gap_ref[3 * j + i : 3 * j + i + 1, :] = row
        mass_ref[...] = expanded(expand_ref[...], sums_ref[0:32, :])


def lagrange_terms(i, j):
    axis = {0: [(1, 1.0)], 1: [(0, 1.0), (1, -1.0), (2, -1.0)], 2: [(2, 1.0)]}
    return [(m, n, p * q) for m, p in axis[i] for n, q in axis[j]]


def expanded(table, moments):
    high = moments.astype(BF16)
    rest = moments - high.astype(F32)
    middle = rest.astype(BF16)
    low = (rest - middle.astype(F32)).astype(BF16)
    return dot(table, high) + dot(table, middle) + dot(table, low)


def owner_kernel(in_ref, expand_ref, force_ref, mass_ref):
    chunks = in_ref.shape[0]
    segments = force_ref.shape[1]
    sums = jnp.zeros((2 * in_ref.shape[1], segments), F32)
    for at in range(0, chunks, 2):
        terms = jnp.concatenate([in_ref[at], in_ref[at + 1]], axis=1)
        hot = one_hot(terms[52:53, :].astype(jnp.int32), segments)
        sums = sums + dot_nt(stack2(terms), hot)
    sums = joined(sums)
    force_ref[...] = sums[0:27, :]
    moments = jnp.concatenate([sums[27:52, :], jnp.zeros((7, segments), F32)], axis=0)
    mass_ref[...] = expanded(expand_ref[...], moments)


def vmem(mib):
    return pltpu.CompilerParams(vmem_limit_bytes=mib << 20)


def from_patches(block):
    patches = lax.axis_size("patch")
    parts = [block]
    for d in range(1, patches):
        parts.append(lax.ppermute(block, "patch", [((i + d) % patches, i) for i in range(patches)]))
    return jnp.concatenate(parts, axis=0)


def from_chips(column):
    segs = lax.axis_size("seg")
    parts = [column]
    for d in range(1, segs // 2):
        parts.append(lax.ppermute(column, "seg", [(i ^ (2 * d), i) for i in range(segs)]))
    return jnp.concatenate(parts, axis=0)


def from_core(plane):
    return lax.ppermute(plane, "seg", [(i ^ 1, i) for i in range(lax.axis_size("seg"))])


def relative_owner(owner):
    patches, segs = lax.axis_size("patch"), lax.axis_size("seg")
    mine = lax.axis_index("seg")
    patch = jnp.mod(owner // segs - lax.axis_index("patch") + patches, patches)
    seg = jnp.bitwise_xor(owner % segs, mine)
    return (seg % 2) * (patches * segs // 2) + (seg // 2) * patches + patch


def shards(
    slave_local,
    owner_route,
    master_local,
    quad_slave,
    quad_master,
    quad_weight,
    slave_coords,
    slave_disp,
    slave_normals,
    multipliers,
    master_coords,
    master_disp,
):
    pairs = slave_local.shape[0]
    segments = slave_coords.shape[2]
    devices = lax.axis_size(AXES)
    cap = 2 * pairs // devices
    steps = pairs // BLOCK

    slave_coords, slave_disp, slave_normals, multipliers, master_coords, master_disp = (
        jnp.transpose(x, (1, 0, 2))
        for x in (slave_coords, slave_disp, slave_normals, multipliers, master_coords, master_disp)
    )
    block = pl.pallas_call(
        table_kernel,
        out_shape=jax.ShapeDtypeStruct((segments // 4, 128), F32),
        scratch_shapes=[pltpu.VMEM((128, segments // 4), F32)],
        name="table",
    )(master_coords, master_disp)
    column = from_patches(block)

    qs, qm, qw = (
        pltpu.with_memory_space_constraint(x, pltpu.HBM)
        for x in (quad_slave.reshape(2 * pairs, 128), quad_master.reshape(2 * pairs, 128), quad_weight)
    )
    sl = slave_local.reshape(1, pairs)
    ml = master_local.reshape(1, pairs)
    owner = owner_route.reshape(1, pairs)
    rows = relative_owner(owner_route.reshape(pairs)) * (segments // 4) + master_local % 128

    planes_spec = pl.BlockSpec((5, 128, BLOCK), lambda i: (0, 0, i))
    row_spec = pl.BlockSpec((1, BLOCK), lambda i: (0, i))

    def whole(x):
        return pl.BlockSpec(x.shape, lambda i: (0,) * len(x.shape))

    def terms_call(first, last, previous):

        def at(spec, dim):
            return pl.BlockSpec(spec, lambda i: tuple(i + first if d == dim else 0 for d in range(2)))

        weight = at((BLOCK, 128), 0)
        quad = at((2 * BLOCK, 128), 0)
        row = at((1, BLOCK), 1)
        return pl.pallas_call(
            terms_kernel,
            grid=(last - first,),
            in_specs=[quad, quad, weight, row, row, whole(multipliers)] + [pl.BlockSpec(memory_space=pl.ANY)] * len(previous),
            out_specs=[
                at((81, BLOCK), 1), at((56, BLOCK), 1), pl.BlockSpec((5, 128, BLOCK), lambda i: (0, 0, i + first)),
            ],
            out_shape=[jax.ShapeDtypeStruct(x, F32) for x in ((81, pairs), (56, pairs), (5, 128, pairs))],
            scratch_shapes=[
                pltpu.VMEM((9, 128, BLOCK), F32),
                pltpu.VMEM((9, 16, BLOCK), F32),
                pltpu.VMEM((64, segments), BF16),
            ],
            input_output_aliases={6 + i: i for i in range(len(previous))},
            compiler_params=vmem(40),
            cost_estimate=pl.CostEstimate(flops=10**9, transcendentals=0, bytes_accessed=15 * 10**6),
            name="terms",
        )(qs, qm, qw, sl, ml, multipliers, *previous)

    cuts = (0, 5 * steps // 16, 12 * steps // 16, steps)
    done = terms_call(cuts[0], cuts[1], ())
    column, done = lax.optimization_barrier((column, done))
    plane = from_chips(column)
    done = terms_call(cuts[1], cuts[2], done)
    plane, done = lax.optimization_barrier((plane, done))
    other = from_core(plane)
    done = terms_call(cuts[2], cuts[3], done)
    other, (coupling, terms, quads) = lax.optimization_barrier((other, done))

    shape = (devices, 56, 128) if cap == 128 else (devices * cap // 256, 56, 256)
    outgoing = pl.pallas_call(
        functools.partial(slots_kernel, devices=devices, cap=cap),
        out_shape=jax.ShapeDtypeStruct(shape, F32),
        scratch_shapes=[pltpu.VMEM((112 * devices * cap // 256, pairs), BF16)],
        compiler_params=vmem(48),
        name="slots",
    )(owner, terms)
    if cap != 128:
        outgoing = outgoing.reshape(shape[0], 56, 256 // cap, cap).transpose(0, 2, 1, 3).reshape(devices, 56, cap)
    incoming = lax.all_to_all(outgoing, AXES, split_axis=0, concat_axis=0, tiled=True)
    if cap != 128:
        incoming = (
            incoming.reshape(devices * cap // 128, 128 // cap, 56, cap).transpose(0, 2, 1, 3).reshape(-1, 56, 128)
        )

    expand = jnp.asarray(expansion(False), BF16)
    hbm = pl.BlockSpec(memory_space=pl.ANY)
    weighted_gap, slave_mass = pl.pallas_call(
        gap_kernel,
        grid=(steps,),
        in_specs=[
            pl.BlockSpec(memory_space=pltpu.SMEM), planes_spec, row_spec, row_spec,
            whole(slave_coords), whole(slave_disp), whole(slave_normals), whole(expand), hbm, hbm,
        ],
        out_specs=[pl.BlockSpec((9, segments), lambda i: (0, 0)), pl.BlockSpec((81, segments), lambda i: (0, 0))],
        out_shape=[jax.ShapeDtypeStruct((9, segments), F32), jax.ShapeDtypeStruct((81, segments), F32)],
        scratch_shapes=[
            pltpu.VMEM((devices * segments // 4, 128), F32),
            pltpu.VMEM((128, segments), BF16),
            pltpu.VMEM((48, segments), F32),
            pltpu.VMEM((48, BLOCK), F32),
            pltpu.VMEM((BLOCK, 128), F32),
            pltpu.SemaphoreType.DMA((2,)),
        ],
        compiler_params=vmem(56),
        cost_estimate=pl.CostEstimate(flops=2 * 10**9, transcendentals=0, bytes_accessed=30 * 10**6),
        name="gap",
    )(rows, quads, sl, ml, slave_coords, slave_disp, slave_normals, expand, plane, other)

    expand = jnp.asarray(expansion(True), BF16)
    force, master_mass = pl.pallas_call(
        owner_kernel,
        out_shape=[jax.ShapeDtypeStruct((27, segments), F32), jax.ShapeDtypeStruct((81, segments), F32)],
        compiler_params=vmem(40),
        name="owner",
    )(incoming, expand)
    return coupling, weighted_gap, slave_mass, force, master_mass


def solution(mesh):
    split = P(AXES)
    table = P(None, None, AXES)
    return jax.shard_map(
        shards,
        mesh=mesh,
        in_specs=(
            split, P(AXES, None), split, P(AXES, None, None), P(AXES, None, None), P(AXES, None),
            table, table, table, table, table, table,
        ),
        out_specs=(P(None, AXES),) * 5,
        check_vma=False,
    )
```

time: 606 us -> 73.5 us (0.12)
  matrix products: 294 us -> 0 us
  local copies, waits for them, and re-layouts: 162 us -> 4.63 us
  other arithmetic: 122 us -> 0.72 us
  Pallas kernels: 0 us -> 46 us
  waiting for transfers between devices: 0.01 us -> 6.3 us
    dot_general x8 -> x0, matrix products: 294 us -> none  [the longest x1 49.3 us: shards(): jnp.einsum('paq,pcq->acp', weighted, slave_shape, precision=highest)]
    gather x11 -> x0, local copies, waits for them, and re-layouts: 77.7 us -> none  [the longest x1 16.6 us: shards(): normals = jnp.take(slave_normals, slave_local, axis=2)]
    scatter-add x3 -> x0, other arithmetic: 50.2 us -> none  [the longest x1 26.4 us: shards(): jax.ops.segment_sum(incoming.T, rows_owned, num_segments=segments)]
    pallas_call x0 -> x7, Pallas kernels: none -> 46 us  [the longest x3 19.5 us: terms_call(): pl.pallas_call(terms_kernel, grid=(last - first,), in_specs=[quad, quad,...]
    transpose x6 -> x0, local copies, waits for them, and re-layouts: 35.8 us -> none  [the longest x1 10.1 us: shards(): jnp.einsum('paq,pbq->abp', weighted, master_shape, precision=highest)]
    mul x5 -> x0, other arithmetic: 30.1 us -> none  [the longest x2 11.3 us: shape_values(): product = second[:, :, None, :] * first[:, None, :, :]]
    scatter x3 -> x0, local copies, waits for them, and re-layouts: 23.3 us -> none  [the longest x1 8.78 us: shards(): jnp.full((devices * cap,), -1, jnp.int32).at[slots].set(master_local)]
    all_to_all x3 -> x1, starting transfers between devices: 19.7 us -> 4.41 us  [shards(): lax.all_to_all(outgoing, AXES, split_axis=0, concat_axis=0, tiled=True)]
  transfers between devices with their start and end apart: 3 -> 8, of which waited for: 0 -> 2; matrix products, arithmetic and copies ran while one was open for 79% -> 1% of each run, Pallas kernels for 0% -> 53%
where the time goes in v1:
time: 73.5 us; the launch traced here: 72.5 us
  Pallas kernels  46 us (63%)
  starting transfers between devices  14.1 us (19%)
  waiting for transfers between devices  6.3 us (9%)
  local copies, waits for them, and re-layouts  4.63 us (6%)
  between operations  0.75 us (1%)
    pallas_call x3, Pallas kernels, terms_call(): pl.pallas_call(terms_kernel, grid=(last - first,), in_specs=[quad, quad,...  19.5 us
    pallas_call x1, Pallas kernels, shards(): pl.pallas_call(gap_kernel, grid=(steps,), in_specs=[pl.BlockSpec(memory_s...  19.1 us
    ppermute x3, starting transfers between devices, from_patches(): lax.ppermute(block, 'patch', [((i + d) % patches, i) for i in range(patch...  6.06 us
    unnamed x20, local copies, waits for them, and re-layouts  4.63 us
    all_to_all x1, starting transfers between devices, shards(): lax.all_to_all(outgoing, AXES, split_axis=0, concat_axis=0, tiled=True)  4.41 us
    all_to_all x1, waiting for transfers between devices, shards(): lax.all_to_all(outgoing, AXES, split_axis=0, concat_axis=0, tiled=True)  3.67 us
    ppermute x3, starting transfers between devices, from_chips(): lax.ppermute(column, 'seg', [(i ^ 2 * d, i) for i in range(segs)])  3.55 us
    pallas_call x1, Pallas kernels, shards(): pl.pallas_call(functools.partial(slots_kernel, devices=devices, cap=cap),...  3.39 us
  transfers between devices with their start and end apart: 8, of which 2 were waited for; matrix products, arithmetic and copies ran while one was open for 1% of the time, Pallas kernels for 53%

profile of v1, /device:TPU:0, one launch (start us, length us, event | category | flops | bytes accessed | tf_op | source)
XLA Modules:
  0.0 72.5 jit_solution(15067234095782232)
XLA Ops:
  0.6 1.7 %table.1 = f32[128,128]{1,0:T(8,128)} custom-call(f32[9,3,512]{2,1,0:T(4,128)} %bitcast.31, f32[9,3,512]{2,1,0:T(4,128)} %bitcast.32), custom_call_target="tpu_custom_call" | custom-call | tf_op jit(solution)/shard_map/table/pallas_call | solution.py:377
  2.3 5.0 %collective-permute-start = (f32[128,128]{1,0:T(8,128)}, f32[128,128]{1,0:T(8,128)S(1)}, u32[]{:S(2)}, u32[]{:S(2)}) collective-permute-start(f32[128,128]{1,0:T(8,128)} %table.1), channel_id=1, source_target_pairs={{8,0},{16,8},{24,16},{0,24},{9,1},{17,9},{25,17},{1,25},{10,2},{18... | collective-permute-start | bytes 196616 | tf_op jit(solution)/shard_map/ppermute | solution.py:329
  7.3 0.0 collective-permute-start.1
  7.3 1.0 %collective-permute-start.2 = (f32[128,128]{1,0:T(8,128)}, f32[128,128]{1,0:T(8,128)S(1)}, u32[]{:S(2)}, u32[]{:S(2)}) collective-permute-start(f32[128,128]{1,0:T(8,128)} %table.1), channel_id=1, source_target_pairs={{24,0},{0,8},{8,16},{16,24},{25,1},{1,9},{9,17},{17,25},{26,2},{2,... | collective-permute-start | bytes 196616 | tf_op jit(solution)/shard_map/ppermute | solution.py:329
  8.4 0.0 copy-start.1
  8.4 0.9 %copy-done.1 = f32[3,9,512]{2,0,1:T(4,128)S(1)} copy-done((f32[3,9,512]{2,0,1:T(4,128)S(1)}, f32[3,9,512]{2,0,1:T(4,128)}, u32[]{:S(2)}) %copy-start.1) | copy-done | bytes 55320
  9.2 0.0 copy-start.2
  9.2 0.7 copy-done.2
  9.9 0.0 copy-start.4
  9.9 0.7 copy-done.4
  10.6 0.0 copy-start.9
  10.6 6.1 %terms.3 = (f32[81,2048]{1,0:T(8,128)}, f32[56,2048]{1,0:T(8,128)S(1)}, f32[5,128,2048]{2,1,0:T(8,128)S(1)}) custom-call(f32[4096,128]{1,0:T(8,128)} %bitcast.25, f32[4096,128]{1,0:T(8,128)} %bitcast.28, f32[2048,128]{1,0:T(8,128)} %w_ref.5, s32[1,2048]{1,0:T(1,128)S(1)} %bitcast.20, s32[1,2048]{1,0:T(1,128)S(1)} %bitcast.16, f32[9,3,512]{2,1,0:T(4,128)S(1)} %bitcast.12), custom_call_target="tpu_custom_call" | custom-call | flops 1000000000 | bytes 15000000 | tf_op jit(solution)/shard_map/terms/pallas_call | solution.py:408
  16.8 0.0 collective-permute-done
  16.8 0.0 collective-permute-done.1
  16.8 0.0 collective-permute-done.2
  16.8 0.0 copy-done.9
  16.8 1.6 %collective-permute-start.3 = (f32[512,128]{1,0:T(8,128)S(1)}, f32[512,128]{1,0:T(8,128)S(1)}, u32[]{:S(2)}, u32[]{:S(2)}) collective-permute-start(f32[512,128]{1,0:T(8,128)S(1)} %pad_maximum_fusion.1), channel_id=1, source_target_pairs={{2,0},{3,1},{0,2},{1,3},{6,4},{7,5},{4,6},{5,7},{10,8},{11,9},{8,1... | collective-permute-start | bytes 786440 | tf_op jit(solution)/shard_map/ppermute | solution.py:337
  18.4 1.5 %collective-permute-start.4 = (f32[512,128]{1,0:T(8,128)S(1)}, f32[512,128]{1,0:T(8,128)S(1)}, u32[]{:S(2)}, u32[]{:S(2)}) collective-permute-start(f32[512,128]{1,0:T(8,128)S(1)} %pad_maximum_fusion.1), channel_id=1, source_target_pairs={{4,0},{5,1},{6,2},{7,3},{0,4},{1,5},{2,6},{3,7},{12,8},{13,9},{14,... | collective-permute-start | bytes 786440 | tf_op jit(solution)/shard_map/ppermute | solution.py:337
  19.9 0.5 collective-permute-start.5
  20.4 7.9 %terms.4 = (f32[81,2048]{1,0:T(8,128)}, f32[56,2048]{1,0:T(8,128)S(1)}, f32[5,128,2048]{2,1,0:T(8,128)S(1)}) custom-call(f32[4096,128]{1,0:T(8,128)} %bitcast.26, f32[4096,128]{1,0:T(8,128)} %bitcast.29, f32[2048,128]{1,0:T(8,128)} %w_ref.5, s32[1,2048]{1,0:T(1,128)S(1)} %bitcast.21, ...), custom_call_target="tpu_custom_call", output_to_operand_aliasing={{0}: (6, {}), {1}: (7, {}), {2}: (8, {})} | custom-call | flops 1000000000 | bytes 15000000 | tf_op jit(solution)/shard_map/terms/pallas_call | solution.py:408
  28.3 0.0 collective-permute-done.3
  28.3 2.6 %collective-permute-done.4 = f32[512,128]{1,0:T(8,128)S(1)} collective-permute-done((f32[512,128]{1,0:T(8,128)S(1)}, f32[512,128]{1,0:T(8,128)S(1)}, u32[]{:S(2)}, u32[]{:S(2)}) %collective-permute-start.4) | collective-permute-done | bytes 262176 | tf_op jit(solution)/shard_map/ppermute | solution.py:337
  30.9 0.0 collective-permute-done.5
  30.9 0.1 pad_maximum_fusion.near_ref
  31.0 0.0 copy-start.7
  31.0 0.0 copy-start.5
  31.0 0.0 copy-start.3
  31.0 0.1 collective-permute-start.6
  31.1 5.5 %terms.5 = (f32[81,2048]{1,0:T(8,128)}, f32[56,2048]{1,0:T(8,128)S(1)}, f32[5,128,2048]{2,1,0:T(8,128)S(1)}) custom-call(f32[4096,128]{1,0:T(8,128)} %bitcast.27, f32[4096,128]{1,0:T(8,128)} %bitcast.30, f32[2048,128]{1,0:T(8,128)} %w_ref.5, s32[1,2048]{1,0:T(1,128)S(1)} %bitcast.22, ...), custom_call_target="tpu_custom_call", output_to_operand_aliasing={{0}: (6, {}), {1}: (7, {}), {2}: (8, {})} | custom-call | flops 1000000000 | bytes 15000000 | tf_op jit(solution)/shard_map/terms/pallas_call | solution.py:408
  36.6 0.0 copy-done.7
  36.6 0.0 copy-start
  36.6 2.3 %copy-done = f32[5,128,2048]{2,1,0:T(8,128)} copy-done((f32[5,128,2048]{2,1,0:T(8,128)}, f32[5,128,2048]{2,1,0:T(8,128)S(1)}, u32[]{:S(2)}) %copy-start) | copy-done | bytes 5242904
  38.9 0.0 collective-permute-done.6.far_ref
  38.9 0.0 copy-start.8
  38.9 0.0 copy-done.5
  38.9 0.0 copy-start.6
  38.9 3.4 %slots.1 = f32[32,56,128]{2,1,0:T(8,128)} custom-call(s32[1,2048]{1,0:T(1,128)S(1)} %bitcast.23, f32[56,2048]{1,0:T(8,128)S(1)} %get-tuple-element.52.terms_ref), custom_call_target="tpu_custom_call" | custom-call | tf_op jit(solution)/shard_map/slots/pallas_call | solution.py:438
  42.3 4.4 %all-to-all-start = ((f32[32,56,128]{2,1,0:T(8,128)}), f32[32,56,128]{2,1,0:T(8,128)S(1)}, u32[]{:S(2)}, u32[]{:S(2)}) async-start(f32[32,56,128]{2,1,0:T(8,128)} %slots.1), calls=%async_computation | async-start | bytes 1835008 | tf_op jit(solution)/shard_map/all_to_all | solution.py:447
  46.7 0.0 copy-done.3
  46.7 0.6 fusion.5.row_ref
  47.4 0.0 copy-done.8
  47.4 19.1 %gap.1 = (f32[9,512]{1,0:T(8,128)}, f32[81,512]{1,0:T(8,128)}) custom-call(s32[2048]{0:T(1024)} %fusion.5.row_ref, f32[5,128,2048]{2,1,0:T(8,128)} %copy-done, s32[1,2048]{1,0:T(1,128)} %bitcast.19, s32[1,2048]{1,0:T(1,128)} %bitcast.15, f32[9,3,512]{2,1,0:T(4,128)} %bitcast.33, f32[9,3,512]{2,1,0:T(4,128)} %bitcast.34, f32[9,3,512]{2,1,0:T(4,128)} %bitcast.35, ...), custom_call_target="tpu_custom_call" | custom-call | flops 2000000000 | bytes 30000000 | tf_op jit(solution)/shard_map/gap/pallas_call | solution.py:455
  66.5 3.7 %all-to-all-done.in_ref = f32[32,56,128]{2,1,0:T(8,128)S(1)} async-done(((f32[32,56,128]{2,1,0:T(8,128)}), f32[32,56,128]{2,1,0:T(8,128)S(1)}, u32[]{:S(2)}, u32[]{:S(2)}) %all-to-all-start) | async-done | bytes 917536 | tf_op jit(solution)/shard_map/all_to_all | solution.py:447
  70.1 0.0 copy-done.6
  70.1 2.4 %owner.1 = (f32[27,512]{1,0:T(8,128)}, f32[81,512]{1,0:T(8,128)}) custom-call(f32[32,56,128]{2,1,0:T(8,128)S(1)} %all-to-all-done.in_ref, bf16[81,32]{1,0:T(8,128)(2,1)S(1)} %copy-done.6), custom_call_target="tpu_custom_call" | custom-call | tf_op jit(solution)/shard_map/owner/pallas_call | solution.py:478
  (1 shorter events, 0.0 us)
Async XLA Ops:
  2.3 14.5 %collective-permute-start = (f32[128,128]{1,0:T(8,128)}, f32[128,128]{1,0:T(8,128)S(1)}, u32[]{:S(2)}, u32[]{:S(2)}) collective-permute-start(f32[128,128]{1,0:T(8,128)} %table.1), channel_id=1, source_target_pairs={{8,0},{16,8},{24,16},{0,24},{9,1},{17,9},{25,17},{1,25},{10,2},{18... | collective-permute-start | bytes 196616 | tf_op jit(solution)/shard_map/ppermute | solution.py:329
  7.3 9.4 %collective-permute-start.1 = (f32[128,128]{1,0:T(8,128)}, f32[128,128]{1,0:T(8,128)S(1)}, u32[]{:S(2)}, u32[]{:S(2)}) collective-permute-start(f32[128,128]{1,0:T(8,128)} %table.1), channel_id=1, source_target_pairs={{16,0},{24,8},{0,16},{8,24},{17,1},{25,9},{1,17},{9,25},{18,2},{26... | collective-permute-start | bytes 196616 | tf_op jit(solution)/shard_map/ppermute | solution.py:329
  7.3 9.4 %collective-permute-start.2 = (f32[128,128]{1,0:T(8,128)}, f32[128,128]{1,0:T(8,128)S(1)}, u32[]{:S(2)}, u32[]{:S(2)}) collective-permute-start(f32[128,128]{1,0:T(8,128)} %table.1), channel_id=1, source_target_pairs={{24,0},{0,8},{8,16},{16,24},{25,1},{1,9},{9,17},{17,25},{26,2},{2,... | collective-permute-start | bytes 196616 | tf_op jit(solution)/shard_map/ppermute | solution.py:329
  8.4 0.9 %copy-start.1 = (f32[3,9,512]{2,0,1:T(4,128)S(1)}, f32[3,9,512]{2,0,1:T(4,128)}, u32[]{:S(2)}) copy-start(f32[3,9,512]{2,0,1:T(4,128)} %param.23) | copy-start | bytes 165892
  9.2 0.7 copy-start.2
  9.9 0.7 copy-start.4
  10.6 6.1 %copy-start.9 = (f32[128,128]{1,0:T(8,128)S(1)}, f32[128,128]{1,0:T(8,128)}, u32[]{:S(2)}) copy-start(f32[128,128]{1,0:T(8,128)} %table.1) | copy-start | bytes 196612
  16.8 11.5 %collective-permute-start.3 = (f32[512,128]{1,0:T(8,128)S(1)}, f32[512,128]{1,0:T(8,128)S(1)}, u32[]{:S(2)}, u32[]{:S(2)}) collective-permute-start(f32[512,128]{1,0:T(8,128)S(1)} %pad_maximum_fusion.1), channel_id=1, source_target_pairs={{2,0},{3,1},{0,2},{1,3},{6,4},{7,5},{4,6},{5,7},{10,8},{11,9},{8,1... | collective-permute-start | bytes 786440 | tf_op jit(solution)/shard_map/ppermute | solution.py:337
  18.4 12.5 %collective-permute-start.4 = (f32[512,128]{1,0:T(8,128)S(1)}, f32[512,128]{1,0:T(8,128)S(1)}, u32[]{:S(2)}, u32[]{:S(2)}) collective-permute-start(f32[512,128]{1,0:T(8,128)S(1)} %pad_maximum_fusion.1), channel_id=1, source_target_pairs={{4,0},{5,1},{6,2},{7,3},{0,4},{1,5},{2,6},{3,7},{12,8},{13,9},{14,... | collective-permute-start | bytes 786440 | tf_op jit(solution)/shard_map/ppermute | solution.py:337
  19.9 11.0 %collective-permute-start.5 = (f32[512,128]{1,0:T(8,128)S(1)}, f32[512,128]{1,0:T(8,128)S(1)}, u32[]{:S(2)}, u32[]{:S(2)}) collective-permute-start(f32[512,128]{1,0:T(8,128)S(1)} %pad_maximum_fusion.1), channel_id=1, source_target_pairs={{6,0},{7,1},{4,2},{5,3},{2,4},{3,5},{0,6},{1,7},{14,8},{15,9},{12,... | collective-permute-start | bytes 786440 | tf_op jit(solution)/shard_map/ppermute | solution.py:337
  31.0 5.6 %copy-start.7 = (f32[2048,128]{1,0:T(8,128)}, f32[2048,128]{1,0:T(8,128)S(1)}, u32[]{:S(2)}) copy-start(f32[2048,128]{1,0:T(8,128)S(1)} %pad_maximum_fusion.near_ref) | copy-start | bytes 3145732
  31.0 7.9 %copy-start.5 = (s32[2048,1]{0,1:T(1,128)S(1)}, s32[2048,1]{0,1:T(1,128)}, u32[]{:S(2)}) copy-start(s32[2048,1]{0,1:T(1,128)} %param.15) | copy-start | bytes 24580
  31.0 15.7 %copy-start.3 = (s32[2048]{0:T(1024)S(1)}, s32[2048]{0:T(1024)}, u32[]{:S(2)}) copy-start(s32[2048]{0:T(1024)} %param.16) | copy-start | bytes 24580
  31.0 7.9 %collective-permute-start.6 = (f32[2048,128]{1,0:T(8,128)S(1)}, f32[2048,128]{1,0:T(8,128)S(1)}, u32[]{:S(2)}, u32[]{:S(2)}) collective-permute-start(f32[2048,128]{1,0:T(8,128)S(1)} %pad_maximum_fusion.near_ref), channel_id=1, source_target_pairs={{1,0},{0,1},{3,2},{2,3},{5,4},{4,5},{7,6},{6,7},{9,8},{8,9},{11,10... | collective-permute-start | bytes 3145736 | tf_op jit(solution)/shard_map/ppermute | solution.py:342
  36.6 2.3 %copy-start = (f32[5,128,2048]{2,1,0:T(8,128)}, f32[5,128,2048]{2,1,0:T(8,128)S(1)}, u32[]{:S(2)}) copy-start(f32[5,128,2048]{2,1,0:T(8,128)S(1)} %get-tuple-element.48.planes_ref) | copy-start | bytes 15728644
  38.9 8.5 %copy-start.8 = (f32[2048,128]{1,0:T(8,128)}, f32[2048,128]{1,0:T(8,128)S(1)}, u32[]{:S(2)}) copy-start(f32[2048,128]{1,0:T(8,128)S(1)} %collective-permute-done.6.far_ref) | copy-start | bytes 3145732
  38.9 31.2 %copy-start.6 = (bf16[81,32]{1,0:T(8,128)(2,1)S(1)}, bf16[81,32]{1,0:T(8,128)(2,1)}, u32[]{:S(2)}) copy-start(bf16[81,32]{1,0:T(8,128)(2,1)} %constant.84.clone.expand_ref) | copy-start | bytes 15556
  42.3 27.8 %all-to-all-start = ((f32[32,56,128]{2,1,0:T(8,128)}), f32[32,56,128]{2,1,0:T(8,128)S(1)}, u32[]{:S(2)}, u32[]{:S(2)}) async-start(f32[32,56,128]{2,1,0:T(8,128)} %slots.1), calls=%async_computation | async-start | bytes 1835008 | tf_op jit(solution)/shard_map/all_to_all | solution.py:447

commit v2 on v1

--- a/solution.py
+++ b/solution.py
@@ -10,6 +10,8 @@
 
 AXES = ("patch", "seg")
 BLOCK = 128
+SUB = 2
+UNROLL = (16, 16, 16)
 F32 = jnp.float32
 BF16 = jnp.bfloat16
 
@@ -31,18 +33,22 @@
     return np.moveaxis(x, 0, along)
 
 
+def power_products():
+    lagrange = np.array([(0, -0.5, 0.5), (1, 0, -1), (0, 0.5, 0.5)], np.float32)
+    return np.array([[np.convolve(p, q) for q in lagrange] for p in lagrange], np.float32)
+
+
 def extra_moments():
     return [(m, n) for m in (3, 4) for n in range(5)] + [(m, n) for m in range(3) for n in (3, 4)]
 
 
-def expansion(plain):
-    axis = axis_products()
+def expansion(powers):
+    axis = power_products() if powers else axis_products()
     table = np.zeros((81, 32), np.float32)
     for b in range(9):
         for c in range(9):
-            both = np.einsum("m,n->mn", axis[b % 3, c % 3], axis[b // 3, c // 3])
-            mixed = reduced(reduced(both, 0), 1)
-            base = both if plain else mixed
+            base = np.einsum("m,n->mn", axis[b % 3, c % 3], axis[b // 3, c // 3])
+            mixed = base if powers else reduced(reduced(base, 0), 1)
             for n in range(3):
                 for m in range(3):
                     table[9 * b + c, 3 * n + m] = base[m, n]
@@ -59,12 +65,17 @@
     return [low, middle, high, low * middle, middle * high]
 
 
-def reduced_rows(x):
+def powers(t):
+    square = t * t
+    return [None, t, square, square * t, square * square]
+
+
+def power_rows(x):
     def along(at, stride):
         out = [None] * 9
         for q in range(3):
             low, middle, high = (at[q * (4 - stride) + stride * i] for i in range(3))
-            for i, block in enumerate((middle, low - middle, high - middle)):
+            for i, block in enumerate((middle, 0.5 * (high - low), 0.5 * (high + low) - middle)):
                 out[q * (4 - stride) + stride * i] = block
         return out
 
@@ -104,8 +115,9 @@
     return jnp.sum(x, axis=0, keepdims=True)
 
 
-def planes(ref):
-    return ref[pl.ds(0, BLOCK, stride=2), :].T, ref[pl.ds(1, BLOCK, stride=2), :].T
+def planes(ref, sub):
+    at = 2 * BLOCK * sub
+    return ref[pl.ds(at, BLOCK, stride=2), :].T, ref[pl.ds(at + 1, BLOCK, stride=2), :].T
 
 
 def product(*factors):
@@ -116,11 +128,22 @@
     return value
 
 
-def extra_rows(w, first, second):
-    first = [None, first[0], first[2], first[3], first[4]]
-    second = [None, second[0], second[2], second[3], second[4]]
+def one_low_high(x):
+    return [None, x[0], x[2], x[3], x[4]]
+
+
+def extra_products(w, first, second):
     weighted = [product(w, x) for x in first]
-    return [total(product(weighted[m], second[n])) for m, n in extra_moments()]
+    return [product(weighted[m], second[n]) for m, n in extra_moments()]
+
+
+def accumulated(count, body, unroll):
+    def step(c, sums):
+        at = c * 8 if isinstance(c, int) else pl.multiple_of(c * 8, 8)
+        return tuple(x + y for x, y in zip(sums, body(pl.ds(at, 8))))
+
+    start = tuple(jnp.zeros((8, BLOCK), F32) for _ in range(count))
+    return lax.fori_loop(0, 16, step, start, unroll=unroll)
 
 
 def fill_rows(table_ref, start, blocks):
@@ -140,36 +163,61 @@
     def _():
         fill_rows(lam_table_ref, 0, [lam_ref[a] for a in range(9)])
 
-    w = w_ref[...].T
-    s, t = planes(qs_ref)
-    u, v = planes(qm_ref)
+    for sub in range(SUB):
+        terms_block(
+            sub, qs_ref, qm_ref, w_ref, sl_ref, ml_ref, coupling_ref, terms_ref, planes_ref, shape_ref, c_ref,
+            lam_table_ref, segments,
+        )
+
+
+def terms_block(
+    sub, qs_ref, qm_ref, w_ref, sl_ref, ml_ref, coupling_ref, terms_ref, planes_ref, shape_ref, c_ref, lam_table_ref,
+    segments,
+):
+    lanes = slice(sub * BLOCK, (sub + 1) * BLOCK)
+    w = w_ref[lanes, :].T
+    s, t = planes(qs_ref, sub)
+    u, v = planes(qm_ref, sub)
     for at, plane in enumerate((s, t, u, v, w)):
-        planes_ref[at] = plane
-    fs, ft, fu, fv = basis(s)[:3], basis(t)[:3], basis(u), basis(v)
-    for b in range(9):
-        shape_ref[b] = fu[b % 3] * fv[b // 3]
-    base = None
-    for a in range(9):
-        weighted = (w * fs[a % 3]) * ft[a // 3]
-        for b in range(9):
-            c_ref[a, b : b + 1, :] = total(weighted * shape_ref[b])
-    lam = joined(dot(lam_table_ref[...], one_hot(sl_ref[...], segments)))
+        planes_ref[sub, at] = plane
+
+    def prepared(rows):
+        s, t, u, v, w = (planes_ref[sub, at, rows, :] for at in range(5))
+        fs, ft, fu, fv = basis(s)[:3], basis(t)[:3], basis(u), basis(v)
+        for j in range(3):
+            for i in range(3):
+                shape_ref[sub, 3 * j + i, rows, :] = fu[i] * fv[j]
+                shape_ref[sub, 9 + 3 * j + i, rows, :] = (w * fs[i]) * ft[j]
+        return extra_products(w, one_low_high(fu), one_low_high(fv))
+
+    extras = accumulated(16, prepared, UNROLL[0])
+    for j in range(3):
+
+        def crossed(rows):
+            master = [shape_ref[sub, b, rows, :] for b in range(9)]
+            return [x * y for x in (shape_ref[sub, 9 + 3 * j + i, rows, :] for i in range(3)) for y in master]
+
+        sums = accumulated(27, crossed, UNROLL[1])
+        for i in range(3):
+            for b in range(9):
+                c_ref[sub, 3 * j + i, b : b + 1, :] = total(sums[9 * i + b])
+    lam = joined(dot(lam_table_ref[...], one_hot(sl_ref[:, lanes], segments)))
     for k in range(3):
-        force = c_ref[0, 0:9, :] * lam[k : k + 1, :]
+        force = c_ref[sub, 0, 0:9, :] * lam[k : k + 1, :]
         for a in range(1, 9):
-            force = force + c_ref[a, 0:9, :] * lam[3 * a + k : 3 * a + k + 1, :]
-        terms_ref[9 * k : 9 * k + 9, :] = force
-    base = c_ref[0, 0:9, :]
-    coupling_ref[0:9, :] = base
+            force = force + c_ref[sub, a, 0:9, :] * lam[3 * a + k : 3 * a + k + 1, :]
+        terms_ref[9 * k : 9 * k + 9, lanes] = force
+    base = c_ref[sub, 0, 0:9, :]
+    coupling_ref[0:9, lanes] = base
     for a in range(1, 9):
-        block = c_ref[a, 0:9, :]
-        coupling_ref[9 * a : 9 * a + 9, :] = block
+        block = c_ref[sub, a, 0:9, :]
+        coupling_ref[9 * a : 9 * a + 9, lanes] = block
         base = base + block
-    terms_ref[27:36, :] = base
-    for at, row in enumerate(extra_rows(w, fu, fv)):
-        terms_ref[36 + at : 37 + at, :] = row
-    terms_ref[52:53, :] = ml_ref[...].astype(F32)
-    terms_ref[53:56, :] = jnp.zeros((3, BLOCK), F32)
+    terms_ref[27:36, lanes] = base
+    for at, x in enumerate(extras):
+        terms_ref[36 + at : 37 + at, lanes] = total(x)
+    terms_ref[52:53, lanes] = ml_ref[:, lanes].astype(F32)
+    terms_ref[53:56, lanes] = jnp.zeros((3, BLOCK), F32)
 
 
 def slots_kernel(owner_ref, terms_ref, out_ref, left_ref, *, devices, cap):
@@ -209,9 +257,10 @@
             out_ref[g] = block
 
 
-def table_kernel(coords_ref, disp_ref, out_ref, rows_ref):
+def table_kernel(coords_ref, disp_ref, owner_ref, local_ref, out_ref, place_ref, rows_ref):
+    place_ref[...] = relative_owner(owner_ref[...]) * out_ref.shape[0] + local_ref[...] % 128
     rows_ref[...] = jnp.zeros_like(rows_ref)
-    for i, block in enumerate(reduced_rows([coords_ref[a] + disp_ref[a] for a in range(9)])):
+    for i, block in enumerate(power_rows([coords_ref[a] + disp_ref[a] for a in range(9)])):
         for c in range(block.shape[1] // 128):
             at = 32 * c + 3 * i
             rows_ref[at : at + 3, :] = block[:, 128 * c : 128 * (c + 1)]
@@ -220,7 +269,7 @@
 
 def gap_kernel(
     row_ref, planes_ref, sl_ref, ml_ref, coords_ref, disp_ref, normals_ref, expand_ref, near_ref, far_ref,
-    gap_ref, mass_ref, table_ref, slave_ref, sums_ref, a_ref, picked_ref, sems,
+    gap_ref, mass_ref, table_ref, slave_ref, sums_ref, a_ref, picked_ref, coef_ref, wide_ref, hot_ref, sems,
 ):
     segments = coords_ref.shape[2]
     step = pl.program_id(0)
@@ -234,53 +283,21 @@
         ]
         for copy in copies:
             copy.start()
-        sums_ref[...] = jnp.zeros_like(sums_ref)
         a_ref[...] = jnp.zeros_like(a_ref)
         slave_ref[...] = jnp.zeros_like(slave_ref)
-        fill_rows(slave_ref, 0, reduced_rows([coords_ref[a] + disp_ref[a] for a in range(9)]))
-        fill_rows(slave_ref, 32, reduced_rows([normals_ref[a] for a in range(9)]))
+        fill_rows(slave_ref, 0, power_rows([coords_ref[a] + disp_ref[a] for a in range(9)]))
+        fill_rows(slave_ref, 32, power_rows([normals_ref[a] for a in range(9)]))
+        hot_ref[...] = one_hot(sl_ref[...], segments)
+        coef_ref[0:64, :] = joined(dot(slave_ref[...], hot_ref[...]))
         for copy in copies:
             copy.wait()
 
-    hot_slave = one_hot(sl_ref[...], segments)
-    slave = joined(dot(slave_ref[...], hot_slave))
-    for p in range(BLOCK):
-        picked_ref[p : p + 1, :] = table_ref[pl.ds(row_ref[step * BLOCK + p], 1), :]
-    picked = picked_ref[...].T
-    quarter = ml_ref[...] // 128
-    position = picked[0:32]
-    for c in range(1, segments // 128):
-        position = jnp.where(quarter == c, picked[32 * c : 32 * c + 32], position)
-
-    s, t, u, v, w = (planes_ref[at] for at in range(5))
-    fs, ft = basis(s), basis(t)
-    fu, fv = basis(u), basis(v)
-
-    def field(coefs, row, first, second):
-        value = None
-        for j in range(3):
-            c = [coefs[row + 9 * j + 3 * i : row + 9 * j + 3 * i + 1] for i in range(3)]
-            part = c[0] + c[1] * first[0] + c[2] * first[2]
-            value = part if j == 0 else value + part * second[0 if j == 1 else 2]
-        return value
-
-    gap = None
-    for k in range(3):
-        normal = field(slave, 32 + k, fs, ft)
-        away = field(position, k, fu, fv) - field(slave, k, fs, ft)
-        gap = normal * away if gap is None else gap + normal * away
-    for n in range(3):
-        for m in range(3):
-            a = 3 * n + m
-            weighted = product(w, (None, fs[0], fs[2])[m], (None, ft[0], ft[2])[n])
-            a_ref[a : a + 1, :] = total(weighted)
-            a_ref[32 + a : 33 + a, :] = total(weighted * gap)
-    for at, row in enumerate(extra_rows(w, fs, ft)):
-        a_ref[9 + at : 10 + at, :] = row
-    sums_ref[...] += joined(dot_nt(stack2(a_ref[...]), hot_slave))
+    for sub in range(SUB):
+        gap_block(sub, step, row_ref, ml_ref, planes_ref, table_ref, picked_ref, coef_ref, wide_ref, a_ref, segments)
 
     @pl.when(step == pl.num_programs(0) - 1)
     def _():
+        sums_ref[...] = joined(dot_nt(stack2(a_ref[...]), hot_ref[...]))
         for j in range(3):
             for i in range(3):
                 row = None
@@ -291,8 +308,48 @@
         mass_ref[...] = expanded(expand_ref[...], sums_ref[0:32, :])
 
 
+def gap_block(sub, step, row_ref, ml_ref, planes_ref, table_ref, picked_ref, coef_ref, wide_ref, a_ref, segments):
+    start = pl.multiple_of((step * SUB + sub) * BLOCK, BLOCK)
+    for p in range(BLOCK):
+        picked_ref[sub, p : p + 1, :] = table_ref[pl.ds(row_ref[0, start + p], 1), :]
+    picked = picked_ref[sub].T
+    quarter = ml_ref[:, pl.ds(start, BLOCK)] // 128
+    position = picked[0:32]
+    for c in range(1, segments // 128):
+        position = jnp.where(quarter == c, picked[32 * c : 32 * c + 32], position)
+    here = pl.ds(start, BLOCK)
+    for row in range(54):
+        at = row if row < 27 else row + 5
+        wide_ref[sub, row] = jnp.broadcast_to(coef_ref[at : at + 1, here], (8, BLOCK))
+    for row in range(27):
+        wide_ref[sub, 54 + row] = jnp.broadcast_to(position[row : row + 1], (8, BLOCK))
+
+    def field(row, first, second):
+        value = None
+        for j in range(3):
+            c = [wide_ref[sub, row + 9 * j + 3 * i] for i in range(3)]
+            part = c[0] + c[1] * first[1] + c[2] * first[2]
+            value = part if j == 0 else value + part * second[j]
+        return value
+
+    def moments(rows):
+        s, t, u, v, w = (planes_ref[sub, at, rows, :] for at in range(5))
+        fs, ft, fu, fv = powers(s), powers(t), powers(u), powers(v)
+        gap = None
+        for k in range(3):
+            part = field(27 + k, fs, ft) * (field(54 + k, fu, fv) - field(k, fs, ft))
+            gap = part if gap is None else gap + part
+        base = [product(w, m, n) for n in ft[:3] for m in fs[:3]]
+        return base + extra_products(w, fs, ft) + [x * gap for x in base]
+
+    sums = accumulated(34, moments, UNROLL[2])
+    for at, x in enumerate(sums):
+        row = at if at < 25 else at + 7
+        a_ref[row : row + 1, here] = total(x)
+
+
 def lagrange_terms(i, j):
-    axis = {0: [(1, 1.0)], 1: [(0, 1.0), (1, -1.0), (2, -1.0)], 2: [(2, 1.0)]}
+    axis = {0: [(1, -0.5), (2, 0.5)], 1: [(0, 1.0), (2, -1.0)], 2: [(1, 0.5), (2, 0.5)]}
     return [(m, n, p * q) for m, p in axis[i] for n, q in axis[j]]
 
 
@@ -368,31 +425,35 @@
     segments = slave_coords.shape[2]
     devices = lax.axis_size(AXES)
     cap = 2 * pairs // devices
-    steps = pairs // BLOCK
+    blocks = pairs // BLOCK
+    steps = blocks // SUB
+    wide = SUB * BLOCK
 
     slave_coords, slave_disp, slave_normals, multipliers, master_coords, master_disp = (
-        jnp.transpose(x, (1, 0, 2))
+        pltpu.with_memory_space_constraint(jnp.transpose(x, (1, 0, 2)), pltpu.HBM)
         for x in (slave_coords, slave_disp, slave_normals, multipliers, master_coords, master_disp)
     )
-    block = pl.pallas_call(
+    qs, qm, qw, sl, ml, owner = (
+        pltpu.with_memory_space_constraint(x, pltpu.HBM)
+        for x in (
+            quad_slave.reshape(2 * pairs, 128),
+            quad_master.reshape(2 * pairs, 128),
+            quad_weight,
+            slave_local.reshape(1, pairs),
+            master_local.reshape(1, pairs),
+            owner_route.reshape(1, pairs),
+        )
+    )
+    block, rows = pl.pallas_call(
         table_kernel,
-        out_shape=jax.ShapeDtypeStruct((segments // 4, 128), F32),
+        out_shape=[jax.ShapeDtypeStruct((segments // 4, 128), F32), jax.ShapeDtypeStruct((1, pairs), jnp.int32)],
         scratch_shapes=[pltpu.VMEM((128, segments // 4), F32)],
         name="table",
-    )(master_coords, master_disp)
+    )(master_coords, master_disp, owner, ml)
     column = from_patches(block)
 
-    qs, qm, qw = (
-        pltpu.with_memory_space_constraint(x, pltpu.HBM)
-        for x in (quad_slave.reshape(2 * pairs, 128), quad_master.reshape(2 * pairs, 128), quad_weight)
-    )
-    sl = slave_local.reshape(1, pairs)
-    ml = master_local.reshape(1, pairs)
-    owner = owner_route.reshape(1, pairs)
-    rows = relative_owner(owner_route.reshape(pairs)) * (segments // 4) + master_local % 128
-
-    planes_spec = pl.BlockSpec((5, 128, BLOCK), lambda i: (0, 0, i))
-    row_spec = pl.BlockSpec((1, BLOCK), lambda i: (0, i))
+    planes_spec = pl.BlockSpec((SUB, 5, 128, BLOCK), lambda i: (i, 0, 0, 0))
+    row_spec = pl.BlockSpec((1, wide), lambda i: (0, i))
 
     def whole(x):
         return pl.BlockSpec(x.shape, lambda i: (0,) * len(x.shape))
@@ -402,44 +463,47 @@
         def at(spec, dim):
             return pl.BlockSpec(spec, lambda i: tuple(i + first if d == dim else 0 for d in range(2)))
 
-        weight = at((BLOCK, 128), 0)
-        quad = at((2 * BLOCK, 128), 0)
-        row = at((1, BLOCK), 1)
+        weight = at((wide, 128), 0)
+        quad = at((2 * wide, 128), 0)
+        row = at((1, wide), 1)
         return pl.pallas_call(
             terms_kernel,
             grid=(last - first,),
             in_specs=[quad, quad, weight, row, row, whole(multipliers)] + [pl.BlockSpec(memory_space=pl.ANY)] * len(previous),
             out_specs=[
-                at((81, BLOCK), 1), at((56, BLOCK), 1), pl.BlockSpec((5, 128, BLOCK), lambda i: (0, 0, i + first)),
+                at((81, wide), 1), at((56, wide), 1), pl.BlockSpec((SUB, 5, 128, BLOCK), lambda i: (i + first, 0, 0, 0)),
             ],
-            out_shape=[jax.ShapeDtypeStruct(x, F32) for x in ((81, pairs), (56, pairs), (5, 128, pairs))],
+            out_shape=[
+                jax.ShapeDtypeStruct((81, pairs), F32),
+                jax.ShapeDtypeStruct((56, pairs), F32),
+                pltpu.HBM((blocks, 5, 128, BLOCK), F32),
+            ],
             scratch_shapes=[
-                pltpu.VMEM((9, 128, BLOCK), F32),
-                pltpu.VMEM((9, 16, BLOCK), F32),
+                pltpu.VMEM((SUB, 18, 128, BLOCK), F32),
+                pltpu.VMEM((SUB, 9, 16, BLOCK), F32),
                 pltpu.VMEM((64, segments), BF16),
             ],
             input_output_aliases={6 + i: i for i in range(len(previous))},
-            compiler_params=vmem(40),
+            compiler_params=vmem(16),
             cost_estimate=pl.CostEstimate(flops=10**9, transcendentals=0, bytes_accessed=15 * 10**6),
             name="terms",
         )(qs, qm, qw, sl, ml, multipliers, *previous)
 
-    cuts = (0, 5 * steps // 16, 12 * steps // 16, steps)
-    done = terms_call(cuts[0], cuts[1], ())
+    cut = 3 * steps // 8
+    done = terms_call(0, cut, ())
     column, done = lax.optimization_barrier((column, done))
     plane = from_chips(column)
-    done = terms_call(cuts[1], cuts[2], done)
-    plane, done = lax.optimization_barrier((plane, done))
+    done = terms_call(cut, steps, done)
+    plane, (coupling, terms, quads) = lax.optimization_barrier((plane, done))
     other = from_core(plane)
-    done = terms_call(cuts[2], cuts[3], done)
-    other, (coupling, terms, quads) = lax.optimization_barrier((other, done))
+    plane, other, quads = (pltpu.with_memory_space_constraint(x, pltpu.HBM) for x in (plane, other, quads))
 
     shape = (devices, 56, 128) if cap == 128 else (devices * cap // 256, 56, 256)
     outgoing = pl.pallas_call(
         functools.partial(slots_kernel, devices=devices, cap=cap),
         out_shape=jax.ShapeDtypeStruct(shape, F32),
         scratch_shapes=[pltpu.VMEM((112 * devices * cap // 256, pairs), BF16)],
-        compiler_params=vmem(48),
+        compiler_params=vmem(24),
         name="slots",
     )(owner, terms)
     if cap != 128:
@@ -450,13 +514,13 @@
             incoming.reshape(devices * cap // 128, 128 // cap, 56, cap).transpose(0, 2, 1, 3).reshape(-1, 56, 128)
         )
 
-    expand = jnp.asarray(expansion(False), BF16)
+    expand = jnp.asarray(expansion(powers=True), BF16)
     hbm = pl.BlockSpec(memory_space=pl.ANY)
     weighted_gap, slave_mass = pl.pallas_call(
         gap_kernel,
         grid=(steps,),
         in_specs=[
-            pl.BlockSpec(memory_space=pltpu.SMEM), planes_spec, row_spec, row_spec,
+            pl.BlockSpec(memory_space=pltpu.SMEM), planes_spec, whole(sl), whole(ml),
             whole(slave_coords), whole(slave_disp), whole(slave_normals), whole(expand), hbm, hbm,
         ],
         out_specs=[pl.BlockSpec((9, segments), lambda i: (0, 0)), pl.BlockSpec((81, segments), lambda i: (0, 0))],
@@ -465,20 +529,23 @@
             pltpu.VMEM((devices * segments // 4, 128), F32),
             pltpu.VMEM((128, segments), BF16),
             pltpu.VMEM((48, segments), F32),
-            pltpu.VMEM((48, BLOCK), F32),
-            pltpu.VMEM((BLOCK, 128), F32),
+            pltpu.VMEM((48, pairs), F32),
+            pltpu.VMEM((SUB, BLOCK, 128), F32),
+            pltpu.VMEM((64, pairs), F32),
+            pltpu.VMEM((SUB, 81, 8, BLOCK), F32),
+            pltpu.VMEM((segments, pairs), BF16),
             pltpu.SemaphoreType.DMA((2,)),
         ],
-        compiler_params=vmem(56),
+        compiler_params=vmem(24),
         cost_estimate=pl.CostEstimate(flops=2 * 10**9, transcendentals=0, bytes_accessed=30 * 10**6),
         name="gap",
     )(rows, quads, sl, ml, slave_coords, slave_disp, slave_normals, expand, plane, other)
 
-    expand = jnp.asarray(expansion(True), BF16)
+    expand = jnp.asarray(expansion(powers=False), BF16)
     force, master_mass = pl.pallas_call(
         owner_kernel,
         out_shape=[jax.ShapeDtypeStruct((27, segments), F32), jax.ShapeDtypeStruct((81, segments), F32)],
-        compiler_params=vmem(40),
+        compiler_params=vmem(16),
         name="owner",
     )(incoming, expand)
     return coupling, weighted_gap, slave_mass, force, master_mass

time: 73.5 us -> 62.8 us (0.85)
  Pallas kernels: 46 us -> 39.6 us
  local copies, waits for them, and re-layouts: 4.63 us -> 1 us
  waiting for transfers between devices: 6.3 us -> 7.58 us
  starting transfers between devices: 14.1 us -> 13.3 us
    pallas_call x3 -> x2, Pallas kernels: 19.5 us -> 15.8 us  [terms_call(): pl.pallas_call(terms_kernel, grid=(last - first,), in_specs=[quad, quad,...]
    unnamed x20 -> x12, local copies, waits for them, and re-layouts: 4.63 us -> 1 us
    pallas_call x1, Pallas kernels: 19.1 us -> 15.6 us  [shards(): pl.pallas_call(gap_kernel, grid=(steps,), in_specs=[pl.BlockSpec(memory_s...]
    ppermute x1, waiting for transfers between devices: 0.01 us -> 2.55 us  [from_core(): lax.ppermute(plane, 'seg', [(i ^ 1, i) for i in range(lax.axis_size('seg'...]
    all_to_all x1, starting transfers between devices: 4.41 us -> 2.64 us  [shards(): lax.all_to_all(outgoing, AXES, split_axis=0, concat_axis=0, tiled=True)]
    ppermute x3, waiting for transfers between devices: 2.62 us -> 0.98 us  [from_chips(): lax.ppermute(column, 'seg', [(i ^ 2 * d, i) for i in range(segs)])]
    ppermute x3, starting transfers between devices: 6.06 us -> 6.96 us  [from_patches(): lax.ppermute(block, 'patch', [((i + d) % patches, i) for i in range(patch...]
    pallas_call x1, Pallas kernels: 3.39 us -> 4.16 us  [shards(): pl.pallas_call(functools.partial(slots_kernel, devices=devices, cap=cap),...]
  transfers between devices with their start and end apart: 8 -> 8, of which waited for: 2 -> 4; matrix products, arithmetic and copies ran while one was open for 1% -> 0% of each run, Pallas kernels for 53% -> 50%
where the time goes in v2:
time: 62.8 us; the launch traced here: 62.3 us
  Pallas kernels  39.6 us (63%)
  starting transfers between devices  13.3 us (21%)
  waiting for transfers between devices  7.58 us (12%)
  local copies, waits for them, and re-layouts  1 us (2%)
  between operations  0.73 us (1%)
    pallas_call x2, Pallas kernels, terms_call(): pl.pallas_call(terms_kernel, grid=(last - first,), in_specs=[quad, quad,...  15.8 us
    pallas_call x1, Pallas kernels, shards(): pl.pallas_call(gap_kernel, grid=(steps,), in_specs=[pl.BlockSpec(memory_s...  15.6 us
    ppermute x3, starting transfers between devices, from_patches(): lax.ppermute(block, 'patch', [((i + d) % patches, i) for i in range(patch...  6.96 us
    pallas_call x1, Pallas kernels, shards(): pl.pallas_call(functools.partial(slots_kernel, devices=devices, cap=cap),...  4.16 us
    all_to_all x1, waiting for transfers between devices, shards(): lax.all_to_all(outgoing, AXES, split_axis=0, concat_axis=0, tiled=True)  4.05 us
    ppermute x3, starting transfers between devices, from_chips(): lax.ppermute(column, 'seg', [(i ^ 2 * d, i) for i in range(segs)])  3.55 us
    all_to_all x1, starting transfers between devices, shards(): lax.all_to_all(outgoing, AXES, split_axis=0, concat_axis=0, tiled=True)  2.64 us
    ppermute x1, waiting for transfers between devices, from_core(): lax.ppermute(plane, 'seg', [(i ^ 1, i) for i in range(lax.axis_size('seg'...  2.55 us
  transfers between devices with their start and end apart: 8, of which 4 were waited for; matrix products, arithmetic and copies ran while one was open for 0% of the time, Pallas kernels for 50%

profile of v2, /device:TPU:0, one launch (start us, length us, event | category | flops | bytes accessed | tf_op | source)
XLA Modules:
  0.0 62.3 jit_solution(17570505058599944835)
XLA Ops:
  0.6 1.7 %table.1 = (f32[128,128]{1,0:T(8,128)}, s32[1,2048]{1,0:T(1,128)}) custom-call(f32[9,3,512]{2,1,0:T(4,128)} %bitcast.21, f32[9,3,512]{2,1,0:T(4,128)} %bitcast.22, s32[1,2048]{1,0:T(1,128)} %bitcast.29, s32[1,2048]{1,0:T(1,128)} %bitcast.17), custom_call_target="tpu_custom_call" | custom-call | tf_op jit(solution)/shard_map/table/pallas_call | solution.py:447
  2.3 0.0 copy-start.5
  2.3 3.0 %collective-permute-start.2 = (f32[128,128]{1,0:T(8,128)}, f32[128,128]{1,0:T(8,128)S(1)}, u32[]{:S(2)}, u32[]{:S(2)}) collective-permute-start(f32[128,128]{1,0:T(8,128)} %get-tuple-element.25), channel_id=1, source_target_pairs={{24,0},{0,8},{8,16},{16,24},{25,1},{1,9},{9,17},{17,25},{26,2},{2,... | collective-permute-start | bytes 196616 | tf_op jit(solution)/shard_map/ppermute | solution.py:386
  5.3 2.6 %collective-permute-start.1 = (f32[128,128]{1,0:T(8,128)}, f32[128,128]{1,0:T(8,128)S(1)}, u32[]{:S(2)}, u32[]{:S(2)}) collective-permute-start(f32[128,128]{1,0:T(8,128)} %get-tuple-element.25), channel_id=1, source_target_pairs={{16,0},{24,8},{0,16},{8,24},{17,1},{25,9},{1,17},{9,25},{18,2},{26... | collective-permute-start | bytes 196616 | tf_op jit(solution)/shard_map/ppermute | solution.py:386
  7.9 1.3 %collective-permute-start = (f32[128,128]{1,0:T(8,128)}, f32[128,128]{1,0:T(8,128)S(1)}, u32[]{:S(2)}, u32[]{:S(2)}) collective-permute-start(f32[128,128]{1,0:T(8,128)} %get-tuple-element.25), channel_id=1, source_target_pairs={{8,0},{16,8},{24,16},{0,24},{9,1},{17,9},{25,17},{1,25},{10,2},{18... | collective-permute-start | bytes 196616 | tf_op jit(solution)/shard_map/ppermute | solution.py:386
  9.3 6.4 %terms.2 = (f32[81,2048]{1,0:T(8,128)}, f32[56,2048]{1,0:T(8,128)S(1)}, f32[16,5,128,128]{3,2,1,0:T(8,128)}) custom-call(f32[4096,128]{1,0:T(8,128)} %bitcast.11, f32[4096,128]{1,0:T(8,128)} %bitcast.13, f32[2048,128]{1,0:T(8,128)} %w_ref.3, s32[1,2048]{1,0:T(1,128)} %bitcast.26, s32[1,2048]{1,0:T(1,128)} %bitcast.18, f32[9,3,512]{2,1,0:T(4,128)} %bitcast.15), custom_call_target="tpu_custom_call" | custom-call | flops 1000000000 | bytes 15000000 | tf_op jit(solution)/shard_map/terms/pallas_call | solution.py:469
  15.7 0.0 collective-permute-done.2
  15.7 0.0 collective-permute-done.1
  15.7 0.0 collective-permute-done
  15.7 0.0 copy-done.5
  15.8 2.5 %collective-permute-start.5 = (f32[512,128]{1,0:T(8,128)S(1)}, f32[512,128]{1,0:T(8,128)S(1)}, u32[]{:S(2)}, u32[]{:S(2)}) collective-permute-start(f32[512,128]{1,0:T(8,128)S(1)} %pad_maximum_fusion.1), channel_id=1, source_target_pairs={{6,0},{7,1},{4,2},{5,3},{2,4},{3,5},{0,6},{1,7},{14,8},{15,9},{12,... | collective-permute-start | bytes 786440 | tf_op jit(solution)/shard_map/ppermute | solution.py:394
  18.3 0.5 collective-permute-start.4
  18.8 0.5 collective-permute-start.3
  19.3 9.3 %terms.3 = (f32[81,2048]{1,0:T(8,128)}, f32[56,2048]{1,0:T(8,128)S(1)}, f32[16,5,128,128]{3,2,1,0:T(8,128)}) custom-call(f32[4096,128]{1,0:T(8,128)} %bitcast.12, f32[4096,128]{1,0:T(8,128)} %bitcast.14, f32[2048,128]{1,0:T(8,128)} %w_ref.3, s32[1,2048]{1,0:T(1,128)} %bitcast.27, ...), custom_call_target="tpu_custom_call", output_to_operand_aliasing={{0}: (6, {}), {1}: (7, {}), {2}: (8, {})} | custom-call | flops 1000000000 | bytes 15000000 | tf_op jit(solution)/shard_map/terms/pallas_call | solution.py:469
  28.7 0.0 copy-start
  28.7 0.0 copy-start.2
  28.7 0.0 collective-permute-done.5
  28.7 0.9 %collective-permute-done.4 = f32[512,128]{1,0:T(8,128)S(1)} collective-permute-done((f32[512,128]{1,0:T(8,128)S(1)}, f32[512,128]{1,0:T(8,128)S(1)}, u32[]{:S(2)}, u32[]{:S(2)}) %collective-permute-start.4) | collective-permute-done | bytes 262176 | tf_op jit(solution)/shard_map/ppermute | solution.py:394
  29.6 0.1 collective-permute-done.3
  29.7 0.1 pad_maximum_fusion.near_ref
  29.7 0.0 copy-start.3
  29.7 0.0 copy-start.1
  29.8 4.2 %slots.1 = f32[32,56,128]{2,1,0:T(8,128)} custom-call(s32[1,2048]{1,0:T(1,128)} %bitcast.30, f32[56,2048]{1,0:T(8,128)S(1)} %get-tuple-element.42.terms_ref), custom_call_target="tpu_custom_call" | custom-call | tf_op jit(solution)/shard_map/slots/pallas_call | solution.py:502
  33.9 2.6 %all-to-all-start = ((f32[32,56,128]{2,1,0:T(8,128)}), f32[32,56,128]{2,1,0:T(8,128)S(1)}, u32[]{:S(2)}, u32[]{:S(2)}) async-start(f32[32,56,128]{2,1,0:T(8,128)} %slots.1), calls=%async_computation | async-start | bytes 1835008 | tf_op jit(solution)/shard_map/all_to_all | solution.py:511
  36.6 0.2 collective-permute-start.6
  36.7 2.5 %collective-permute-done.6.far_ref = f32[2048,128]{1,0:T(8,128)S(1)} collective-permute-done((f32[2048,128]{1,0:T(8,128)S(1)}, f32[2048,128]{1,0:T(8,128)S(1)}, u32[]{:S(2)}, u32[]{:S(2)}) %collective-permute-start.6) | collective-permute-done | bytes 1048608 | tf_op jit(solution)/shard_map/ppermute | solution.py:399
  39.3 0.0 copy-start.4
  39.3 0.0 copy-done.3
  39.3 1.0 %copy-done.4 = f32[2048,128]{1,0:T(8,128)} copy-done((f32[2048,128]{1,0:T(8,128)}, f32[2048,128]{1,0:T(8,128)S(1)}, u32[]{:S(2)}) %copy-start.4) | copy-done | bytes 1048600
  40.3 0.0 copy-done
  40.3 0.0 copy-done.2
  40.3 15.6 %gap.1 = (f32[9,512]{1,0:T(8,128)}, f32[81,512]{1,0:T(8,128)}) custom-call(s32[1,2048]{1,0:T(1,128)S(1)} %copy-done.2, f32[16,5,128,128]{3,2,1,0:T(8,128)} %get-tuple-element.38.planes_ref, s32[1,2048]{1,0:T(1,128)} %bitcast.28, s32[1,2048]{1,0:T(1,128)} %bitcast.20, f32[9,3,512]{2,1,0:T(4,128)} %bitcast.23, f32[9,3,512]{2,1,0:T(4,128)} %bitcast.24, ...), custom_call_target="tpu_custom_call" | custom-call | flops 2000000000 | bytes 30000000 | tf_op jit(solution)/shard_map/gap/pallas_call | solution.py:519
  55.9 4.0 %all-to-all-done.in_ref = f32[32,56,128]{2,1,0:T(8,128)S(1)} async-done(((f32[32,56,128]{2,1,0:T(8,128)}), f32[32,56,128]{2,1,0:T(8,128)S(1)}, u32[]{:S(2)}, u32[]{:S(2)}) %all-to-all-start) | async-done | bytes 917536 | tf_op jit(solution)/shard_map/all_to_all | solution.py:511
  60.0 0.0 copy-done.1
  60.0 2.4 %owner.1 = (f32[27,512]{1,0:T(8,128)}, f32[81,512]{1,0:T(8,128)}) custom-call(f32[32,56,128]{2,1,0:T(8,128)S(1)} %all-to-all-done.in_ref, bf16[81,32]{1,0:T(8,128)(2,1)S(1)} %copy-done.1), custom_call_target="tpu_custom_call" | custom-call | tf_op jit(solution)/shard_map/owner/pallas_call | solution.py:545
  (1 shorter events, 0.0 us)
Async XLA Ops:
  2.3 13.4 %copy-start.5 = (f32[128,128]{1,0:T(8,128)S(1)}, f32[128,128]{1,0:T(8,128)}, u32[]{:S(2)}) copy-start(f32[128,128]{1,0:T(8,128)} %get-tuple-element.25) | copy-start | bytes 196612
  2.3 13.4 %collective-permute-start.2 = (f32[128,128]{1,0:T(8,128)}, f32[128,128]{1,0:T(8,128)S(1)}, u32[]{:S(2)}, u32[]{:S(2)}) collective-permute-start(f32[128,128]{1,0:T(8,128)} %get-tuple-element.25), channel_id=1, source_target_pairs={{24,0},{0,8},{8,16},{16,24},{25,1},{1,9},{9,17},{17,25},{26,2},{2,... | collective-permute-start | bytes 196616 | tf_op jit(solution)/shard_map/ppermute | solution.py:386
  5.3 10.4 %collective-permute-start.1 = (f32[128,128]{1,0:T(8,128)}, f32[128,128]{1,0:T(8,128)S(1)}, u32[]{:S(2)}, u32[]{:S(2)}) collective-permute-start(f32[128,128]{1,0:T(8,128)} %get-tuple-element.25), channel_id=1, source_target_pairs={{16,0},{24,8},{0,16},{8,24},{17,1},{25,9},{1,17},{9,25},{18,2},{26... | collective-permute-start | bytes 196616 | tf_op jit(solution)/shard_map/ppermute | solution.py:386
  7.9 7.8 %collective-permute-start = (f32[128,128]{1,0:T(8,128)}, f32[128,128]{1,0:T(8,128)S(1)}, u32[]{:S(2)}, u32[]{:S(2)}) collective-permute-start(f32[128,128]{1,0:T(8,128)} %get-tuple-element.25), channel_id=1, source_target_pairs={{8,0},{16,8},{24,16},{0,24},{9,1},{17,9},{25,17},{1,25},{10,2},{18... | collective-permute-start | bytes 196616 | tf_op jit(solution)/shard_map/ppermute | solution.py:386
  15.8 12.9 %collective-permute-start.5 = (f32[512,128]{1,0:T(8,128)S(1)}, f32[512,128]{1,0:T(8,128)S(1)}, u32[]{:S(2)}, u32[]{:S(2)}) collective-permute-start(f32[512,128]{1,0:T(8,128)S(1)} %pad_maximum_fusion.1), channel_id=1, source_target_pairs={{6,0},{7,1},{4,2},{5,3},{2,4},{3,5},{0,6},{1,7},{14,8},{15,9},{12,... | collective-permute-start | bytes 786440 | tf_op jit(solution)/shard_map/ppermute | solution.py:394
  18.3 11.3 %collective-permute-start.4 = (f32[512,128]{1,0:T(8,128)S(1)}, f32[512,128]{1,0:T(8,128)S(1)}, u32[]{:S(2)}, u32[]{:S(2)}) collective-permute-start(f32[512,128]{1,0:T(8,128)S(1)} %pad_maximum_fusion.1), channel_id=1, source_target_pairs={{4,0},{5,1},{6,2},{7,3},{0,4},{1,5},{2,6},{3,7},{12,8},{13,9},{14,... | collective-permute-start | bytes 786440 | tf_op jit(solution)/shard_map/ppermute | solution.py:394
  18.8 10.9 %collective-permute-start.3 = (f32[512,128]{1,0:T(8,128)S(1)}, f32[512,128]{1,0:T(8,128)S(1)}, u32[]{:S(2)}, u32[]{:S(2)}) collective-permute-start(f32[512,128]{1,0:T(8,128)S(1)} %pad_maximum_fusion.1), channel_id=1, source_target_pairs={{2,0},{3,1},{0,2},{1,3},{6,4},{7,5},{4,6},{5,7},{10,8},{11,9},{8,1... | collective-permute-start | bytes 786440 | tf_op jit(solution)/shard_map/ppermute | solution.py:394
  28.7 11.6 %copy-start = (bf16[81,32]{1,0:T(8,128)(2,1)S(1)}, bf16[81,32]{1,0:T(8,128)(2,1)}, u32[]{:S(2)}) copy-start(bf16[81,32]{1,0:T(8,128)(2,1)} %constant.4.clone.expand_ref) | copy-start | bytes 15556
  28.7 11.6 %copy-start.2 = (s32[1,2048]{1,0:T(1,128)S(1)}, s32[1,2048]{1,0:T(1,128)}, u32[]{:S(2)}) copy-start(s32[1,2048]{1,0:T(1,128)} %get-tuple-element.37.row_ref) | copy-start | bytes 24580
  29.7 9.6 %copy-start.3 = (f32[2048,128]{1,0:T(8,128)}, f32[2048,128]{1,0:T(8,128)S(1)}, u32[]{:S(2)}) copy-start(f32[2048,128]{1,0:T(8,128)S(1)} %pad_maximum_fusion.near_ref) | copy-start | bytes 3145732
  29.7 30.2 %copy-start.1 = (bf16[81,32]{1,0:T(8,128)(2,1)S(1)}, bf16[81,32]{1,0:T(8,128)(2,1)}, u32[]{:S(2)}) copy-start(bf16[81,32]{1,0:T(8,128)(2,1)} %constant.5.clone.expand_ref) | copy-start | bytes 15556
  33.9 26.1 %all-to-all-start = ((f32[32,56,128]{2,1,0:T(8,128)}), f32[32,56,128]{2,1,0:T(8,128)S(1)}, u32[]{:S(2)}, u32[]{:S(2)}) async-start(f32[32,56,128]{2,1,0:T(8,128)} %slots.1), calls=%async_computation | async-start | bytes 1835008 | tf_op jit(solution)/shard_map/all_to_all | solution.py:511
  36.6 2.7 %collective-permute-start.6 = (f32[2048,128]{1,0:T(8,128)S(1)}, f32[2048,128]{1,0:T(8,128)S(1)}, u32[]{:S(2)}, u32[]{:S(2)}) collective-permute-start(f32[2048,128]{1,0:T(8,128)S(1)} %pad_maximum_fusion.near_ref), channel_id=1, source_target_pairs={{1,0},{0,1},{3,2},{2,3},{5,4},{4,5},{7,6},{6,7},{9,8},{8,9},{11,10... | collective-permute-start | bytes 3145736 | tf_op jit(solution)/shard_map/ppermute | solution.py:399
  39.3 1.0 %copy-start.4 = (f32[2048,128]{1,0:T(8,128)}, f32[2048,128]{1,0:T(8,128)S(1)}, u32[]{:S(2)}) copy-start(f32[2048,128]{1,0:T(8,128)S(1)} %collective-permute-done.6.far_ref) | copy-start | bytes 3145732

commit v3 on v2

--- a/solution.py
+++ b/solution.py
@@ -11,58 +11,41 @@
 AXES = ("patch", "seg")
 BLOCK = 128
 SUB = 2
+GAP_FLOPS = 2 * 10**9
+GAP_BYTES = 60 * 10**6
 UNROLL = (16, 16, 16)
 F32 = jnp.float32
 BF16 = jnp.bfloat16
 
 
-def axis_products():
-    axis = np.zeros((3, 3, 5), np.float32)
-    axis[0, 0] = (1, 0, 0, -0.75, 0.25)
-    axis[0, 1] = axis[1, 0] = (0, 0, 0, 1, 0)
-    axis[0, 2] = axis[2, 0] = (0, 0, 0, -0.25, -0.25)
-    axis[1, 1] = (0, 1, 0, -1, -1)
-    axis[1, 2] = axis[2, 1] = (0, 0, 0, 0, 1)
-    axis[2, 2] = (0, 0, 1, 0.25, -0.75)
-    return axis
-
-
-def reduced(x, along):
-    x = np.moveaxis(x, along, 0)
-    x = np.concatenate([x[1:2], x[0:1] - x[1:2], x[2:3] - x[1:2], x[3:]], axis=0)
-    return np.moveaxis(x, 0, along)
+LAGRANGE = np.array([(0, -0.5, 0.5), (1, 0, -1), (0, 0.5, 0.5)], np.float32)
+
+
+def from_powers():
+    nodes = np.einsum("jn,im->jinm", LAGRANGE, LAGRANGE).reshape(9, 9)
+    table = np.zeros((88, 96), np.float32)
+    for at, column in enumerate(np.einsum("ac,bd->cdab", nodes, nodes).reshape(81, 81)):
+        table[:81, 32 * (at // 27) + at % 27] = column
+    return table
 
 
 def power_products():
-    lagrange = np.array([(0, -0.5, 0.5), (1, 0, -1), (0, 0.5, 0.5)], np.float32)
-    return np.array([[np.convolve(p, q) for q in lagrange] for p in lagrange], np.float32)
+    return np.array([[np.convolve(p, q) for q in LAGRANGE] for p in LAGRANGE], np.float32)
 
 
 def extra_moments():
     return [(m, n) for m in (3, 4) for n in range(5)] + [(m, n) for m in range(3) for n in (3, 4)]
 
 
-def expansion(powers):
-    axis = power_products() if powers else axis_products()
+def expansion():
+    axis = power_products()
     table = np.zeros((81, 32), np.float32)
+    columns = [(m, n) for n in range(3) for m in range(3)] + extra_moments()
     for b in range(9):
         for c in range(9):
-            base = np.einsum("m,n->mn", axis[b % 3, c % 3], axis[b // 3, c // 3])
-            mixed = base if powers else reduced(reduced(base, 0), 1)
-            for n in range(3):
-                for m in range(3):
-                    table[9 * b + c, 3 * n + m] = base[m, n]
-            for at, (m, n) in enumerate(extra_moments()):
-                table[9 * b + c, 9 + at] = mixed[m, n]
+            for at, (m, n) in enumerate(columns):
+                table[9 * b + c, at] = axis[b % 3, c % 3, m] * axis[b // 3, c // 3, n]
     return table
-
-
-def basis(t):
-    square = t * t
-    low = 0.5 * (square - t)
-    middle = 1.0 - square
-    high = low + t
-    return [low, middle, high, low * middle, middle * high]
 
 
 def powers(t):
@@ -115,6 +98,27 @@
     return jnp.sum(x, axis=0, keepdims=True)
 
 
+def merged(x, y, distance):
+    rows = lax.broadcasted_iota(jnp.int32, (8, BLOCK), 0)
+    first = (rows & distance) == 0
+    if distance == 4:
+        return jnp.where(first, x, y) + pltpu.roll(jnp.where(first, y, x), 4, 0)
+    return jnp.where(first, x, y) + jnp.where(first, pltpu.roll(x, 8 - distance, 0), pltpu.roll(y, distance, 0))
+
+
+def put_totals(ref, row, lanes, sums):
+    for at in range(0, len(sums), 8):
+        part = list(sums[at : at + 8])
+        if len(part) == 1:
+            ref[row + at : row + at + 1, lanes] = total(part[0])
+            continue
+        count = len(part)
+        part = part + part[:1] * (8 - count)
+        for distance in (4, 2, 1):
+            part = [merged(part[k], part[k + distance], distance) for k in range(distance)]
+        ref[row + at : row + at + count, lanes] = part[0][:count]
+
+
 def planes(ref, sub):
     at = 2 * BLOCK * sub
     return ref[pl.ds(at, BLOCK, stride=2), :].T, ref[pl.ds(at + 1, BLOCK, stride=2), :].T
@@ -126,10 +130,6 @@
         if x is not None:
             value = x if value is None else value * x
     return value
-
-
-def one_low_high(x):
-    return [None, x[0], x[2], x[3], x[4]]
 
 
 def extra_products(w, first, second):
@@ -155,69 +155,59 @@
         table_ref[at + half : at + half + 3, :] = low
 
 
-def terms_kernel(qs_ref, qm_ref, w_ref, sl_ref, ml_ref, lam_ref, *rest):
-    coupling_ref, terms_ref, planes_ref, shape_ref, c_ref, lam_table_ref = rest[-6:]
+def terms_kernel(qs_ref, qm_ref, w_ref, sl_ref, ml_ref, lam_ref, couple_ref, *rest):
+    coupling_ref, terms_ref, planes_ref, shape_ref, c_ref, block_ref, lam_table_ref = rest[-7:]
     segments = lam_ref.shape[2]
 
     @pl.when(pl.program_id(0) == 0)
     def _():
+        c_ref[...] = jnp.zeros_like(c_ref)
         fill_rows(lam_table_ref, 0, [lam_ref[a] for a in range(9)])
 
     for sub in range(SUB):
-        terms_block(
-            sub, qs_ref, qm_ref, w_ref, sl_ref, ml_ref, coupling_ref, terms_ref, planes_ref, shape_ref, c_ref,
-            lam_table_ref, segments,
-        )
-
-
-def terms_block(
-    sub, qs_ref, qm_ref, w_ref, sl_ref, ml_ref, coupling_ref, terms_ref, planes_ref, shape_ref, c_ref, lam_table_ref,
-    segments,
-):
+        w = w_ref[sub * BLOCK : (sub + 1) * BLOCK, :].T
+        for at, plane in enumerate((*planes(qs_ref, sub), *planes(qm_ref, sub), w)):
+            planes_ref[sub, at] = plane
+    lam = joined(dot(lam_table_ref[...], one_hot(sl_ref[...], segments)))
+    for sub in range(SUB):
+        crossed_sums(sub, planes_ref, shape_ref, c_ref, terms_ref)
+    moments = c_ref[...]
+    coupling = expanded(couple_ref[...], moments)
+    coupling_ref[...] = coupling[0:81]
+    for a in range(9):
+        block_ref[a, 0:9, :] = coupling[9 * a : 9 * a + 9]
+    for k in range(3):
+        force = block_ref[0, 0:9, :] * lam[k : k + 1, :]
+        for a in range(1, 9):
+            force = force + block_ref[a, 0:9, :] * lam[3 * a + k : 3 * a + k + 1, :]
+        terms_ref[9 * k : 9 * k + 9, :] = force
+    terms_ref[27:36, :] = moments[0:9]
+    terms_ref[52:53, :] = ml_ref[...].astype(F32)
+    terms_ref[53:56, :] = jnp.zeros((3, SUB * BLOCK), F32)
+
+
+def crossed_sums(sub, planes_ref, shape_ref, c_ref, terms_ref):
     lanes = slice(sub * BLOCK, (sub + 1) * BLOCK)
-    w = w_ref[lanes, :].T
-    s, t = planes(qs_ref, sub)
-    u, v = planes(qm_ref, sub)
-    for at, plane in enumerate((s, t, u, v, w)):
-        planes_ref[sub, at] = plane
 
     def prepared(rows):
         s, t, u, v, w = (planes_ref[sub, at, rows, :] for at in range(5))
-        fs, ft, fu, fv = basis(s)[:3], basis(t)[:3], basis(u), basis(v)
+        fs, ft, fu, fv = powers(s), powers(t), powers(u), powers(v)
         for j in range(3):
             for i in range(3):
-                shape_ref[sub, 3 * j + i, rows, :] = fu[i] * fv[j]
-                shape_ref[sub, 9 + 3 * j + i, rows, :] = (w * fs[i]) * ft[j]
-        return extra_products(w, one_low_high(fu), one_low_high(fv))
-
-    extras = accumulated(16, prepared, UNROLL[0])
+                if i + j > 0:
+                    shape_ref[sub, 3 * j + i, rows, :] = product(fu[i], fv[j])
+                shape_ref[sub, 9 + 3 * j + i, rows, :] = product(w, fs[i], ft[j])
+        return extra_products(w, fu, fv)
+
+    put_totals(terms_ref, 36, lanes, accumulated(16, prepared, UNROLL[0]))
     for j in range(3):
 
         def crossed(rows):
-            master = [shape_ref[sub, b, rows, :] for b in range(9)]
-            return [x * y for x in (shape_ref[sub, 9 + 3 * j + i, rows, :] for i in range(3)) for y in master]
-
-        sums = accumulated(27, crossed, UNROLL[1])
-        for i in range(3):
-            for b in range(9):
-                c_ref[sub, 3 * j + i, b : b + 1, :] = total(sums[9 * i + b])
-    lam = joined(dot(lam_table_ref[...], one_hot(sl_ref[:, lanes], segments)))
-    for k in range(3):
-        force = c_ref[sub, 0, 0:9, :] * lam[k : k + 1, :]
-        for a in range(1, 9):
-            force = force + c_ref[sub, a, 0:9, :] * lam[3 * a + k : 3 * a + k + 1, :]
-        terms_ref[9 * k : 9 * k + 9, lanes] = force
-    base = c_ref[sub, 0, 0:9, :]
-    coupling_ref[0:9, lanes] = base
-    for a in range(1, 9):
-        block = c_ref[sub, a, 0:9, :]
-        coupling_ref[9 * a : 9 * a + 9, lanes] = block
-        base = base + block
-    terms_ref[27:36, lanes] = base
-    for at, x in enumerate(extras):
-        terms_ref[36 + at : 37 + at, lanes] = total(x)
-    terms_ref[52:53, lanes] = ml_ref[:, lanes].astype(F32)
-    terms_ref[53:56, lanes] = jnp.zeros((3, BLOCK), F32)
+            master = [None] + [shape_ref[sub, b, rows, :] for b in range(1, 9)]
+            slave = [shape_ref[sub, 9 + 3 * j + i, rows, :] for i in range(3)]
+            return [product(x, y) for x in slave for y in master]
+
+        put_totals(c_ref, 32 * j, lanes, accumulated(27, crossed, UNROLL[1]))
 
 
 def slots_kernel(owner_ref, terms_ref, out_ref, left_ref, *, devices, cap):
@@ -343,9 +333,8 @@
         return base + extra_products(w, fs, ft) + [x * gap for x in base]
 
     sums = accumulated(34, moments, UNROLL[2])
-    for at, x in enumerate(sums):
-        row = at if at < 25 else at + 7
-        a_ref[row : row + 1, here] = total(x)
+    put_totals(a_ref, 0, here, sums[:25])
+    put_totals(a_ref, 32, here, sums[25:])
 
 
 def lagrange_terms(i, j):
@@ -364,11 +353,17 @@
 def owner_kernel(in_ref, expand_ref, force_ref, mass_ref):
     chunks = in_ref.shape[0]
     segments = force_ref.shape[1]
-    sums = jnp.zeros((2 * in_ref.shape[1], segments), F32)
+    rows = 2 * in_ref.shape[1]
+    half = segments // 2
+    sums = jnp.zeros((2 * rows, half), F32)
     for at in range(0, chunks, 2):
         terms = jnp.concatenate([in_ref[at], in_ref[at + 1]], axis=1)
-        hot = one_hot(terms[52:53, :].astype(jnp.int32), segments)
-        sums = sums + dot_nt(stack2(terms), hot)
+        local = terms[52:53, :].astype(jnp.int32)
+        both = stack2(terms)
+        upper = jnp.where(local >= half, 1.0, 0.0).astype(BF16)
+        left = jnp.concatenate([both * (1 - upper), both * upper], axis=0)
+        sums = sums + dot_nt(left, one_hot(local % half, half))
+    sums = jnp.concatenate([sums[:rows], sums[rows:]], axis=1)
     sums = joined(sums)
     force_ref[...] = sums[0:27, :]
     moments = jnp.concatenate([sums[27:52, :], jnp.zeros((7, segments), F32)], axis=0)
@@ -392,7 +387,7 @@
     parts = [column]
     for d in range(1, segs // 2):
         parts.append(lax.ppermute(column, "seg", [(i ^ (2 * d), i) for i in range(segs)]))
-    return jnp.concatenate(parts, axis=0)
+    return jnp.concatenate(lax.optimization_barrier(parts), axis=0)
 
 
 def from_core(plane):
@@ -458,6 +453,8 @@
     def whole(x):
         return pl.BlockSpec(x.shape, lambda i: (0,) * len(x.shape))
 
+    couple = pltpu.with_memory_space_constraint(jnp.asarray(from_powers(), BF16), pltpu.HBM)
+
     def terms_call(first, last, previous):
 
         def at(spec, dim):
@@ -469,7 +466,7 @@
         return pl.pallas_call(
             terms_kernel,
             grid=(last - first,),
-            in_specs=[quad, quad, weight, row, row, whole(multipliers)] + [pl.BlockSpec(memory_space=pl.ANY)] * len(previous),
+            in_specs=[quad, quad, weight, row, row, whole(multipliers), whole(couple)] + [pl.BlockSpec(memory_space=pl.ANY)] * len(previous),
             out_specs=[
                 at((81, wide), 1), at((56, wide), 1), pl.BlockSpec((SUB, 5, 128, BLOCK), lambda i: (i + first, 0, 0, 0)),
             ],
@@ -480,23 +477,21 @@
             ],
             scratch_shapes=[
                 pltpu.VMEM((SUB, 18, 128, BLOCK), F32),
-                pltpu.VMEM((SUB, 9, 16, BLOCK), F32),
+                pltpu.VMEM((96, wide), F32),
+                pltpu.VMEM((9, 16, wide), F32),
                 pltpu.VMEM((64, segments), BF16),
             ],
-            input_output_aliases={6 + i: i for i in range(len(previous))},
+            input_output_aliases={7 + i: i for i in range(len(previous))},
             compiler_params=vmem(16),
             cost_estimate=pl.CostEstimate(flops=10**9, transcendentals=0, bytes_accessed=15 * 10**6),
             name="terms",
-        )(qs, qm, qw, sl, ml, multipliers, *previous)
-
-    cut = 3 * steps // 8
-    done = terms_call(0, cut, ())
-    column, done = lax.optimization_barrier((column, done))
+        )(qs, qm, qw, sl, ml, multipliers, couple, *previous)
+
+    done = terms_call(0, steps, ())
+    column, (coupling, terms, quads) = lax.optimization_barrier((column, done))
     plane = from_chips(column)
-    done = terms_call(cut, steps, done)
-    plane, (coupling, terms, quads) = lax.optimization_barrier((plane, done))
     other = from_core(plane)
-    plane, other, quads = (pltpu.with_memory_space_constraint(x, pltpu.HBM) for x in (plane, other, quads))
+    quads = pltpu.with_memory_space_constraint(quads, pltpu.HBM)
 
     shape = (devices, 56, 128) if cap == 128 else (devices * cap // 256, 56, 256)
     outgoing = pl.pallas_call(
@@ -514,7 +509,7 @@
             incoming.reshape(devices * cap // 128, 128 // cap, 56, cap).transpose(0, 2, 1, 3).reshape(-1, 56, 128)
         )
 
-    expand = jnp.asarray(expansion(powers=True), BF16)
+    expand = jnp.asarray(expansion(), BF16)
     hbm = pl.BlockSpec(memory_space=pl.ANY)
     weighted_gap, slave_mass = pl.pallas_call(
         gap_kernel,
@@ -537,11 +532,10 @@
             pltpu.SemaphoreType.DMA((2,)),
         ],
         compiler_params=vmem(24),
-        cost_estimate=pl.CostEstimate(flops=2 * 10**9, transcendentals=0, bytes_accessed=30 * 10**6),
+        cost_estimate=pl.CostEstimate(flops=GAP_FLOPS, transcendentals=0, bytes_accessed=GAP_BYTES),
         name="gap",
     )(rows, quads, sl, ml, slave_coords, slave_disp, slave_normals, expand, plane, other)
 
-    expand = jnp.asarray(expansion(powers=False), BF16)
     force, master_mass = pl.pallas_call(
         owner_kernel,
         out_shape=[jax.ShapeDtypeStruct((27, segments), F32), jax.ShapeDtypeStruct((81, segments), F32)],

time: 62.8 us -> 59.7 us (0.951)
  Pallas kernels: 39.6 us -> 36.7 us
  local copies, waits for them, and re-layouts: 1 us -> 0.09 us
  waiting for transfers between devices: 7.58 us -> 8.21 us
    ppermute x3, waiting for transfers between devices: 0.98 us -> 4.29 us  [from_chips(): lax.ppermute(column, 'seg', [(i ^ 2 * d, i) for i in range(segs)])]
    all_to_all x1, waiting for transfers between devices: 4.05 us -> 1.26 us  [shards(): lax.all_to_all(outgoing, AXES, split_axis=0, concat_axis=0, tiled=True)]
    pallas_call x2 -> x1, Pallas kernels: 15.8 us -> 14.2 us  [terms_call(): pl.pallas_call(terms_kernel, grid=(last - first,), in_specs=[quad, quad,...]
    unnamed x12 -> x9, local copies, waits for them, and re-layouts: 1 us -> 0.07 us
  transfers between devices with their start and end apart: 8 -> 8, of which waited for: 4 -> 4; matrix products, arithmetic and copies ran while one was open for 0% -> 0% of each run, Pallas kernels for 50% -> 56%
where the time goes in v3:
time: 59.7 us; the launch traced here: 59.3 us
  Pallas kernels  36.7 us (61%)
  starting transfers between devices  13.5 us (23%)
  waiting for transfers between devices  8.21 us (14%)
  between operations  0.73 us (1%)
    pallas_call x1, Pallas kernels, shards(): pl.pallas_call(gap_kernel, grid=(steps,), in_specs=[pl.BlockSpec(memory_s...  15 us
    pallas_call x1, Pallas kernels, terms_call(): pl.pallas_call(terms_kernel, grid=(last - first,), in_specs=[quad, quad,...  14.2 us
    ppermute x3, starting transfers between devices, from_patches(): lax.ppermute(block, 'patch', [((i + d) % patches, i) for i in range(patch...  6.96 us
    ppermute x3, waiting for transfers between devices, from_chips(): lax.ppermute(column, 'seg', [(i ^ 2 * d, i) for i in range(segs)])  4.29 us
    pallas_call x1, Pallas kernels, shards(): pl.pallas_call(functools.partial(slots_kernel, devices=devices, cap=cap),...  4.06 us
    ppermute x3, starting transfers between devices, from_chips(): lax.ppermute(column, 'seg', [(i ^ 2 * d, i) for i in range(segs)])  3.55 us
    all_to_all x1, starting transfers between devices, shards(): lax.all_to_all(outgoing, AXES, split_axis=0, concat_axis=0, tiled=True)  2.93 us
    ppermute x1, waiting for transfers between devices, from_core(): lax.ppermute(plane, 'seg', [(i ^ 1, i) for i in range(lax.axis_size('seg'...  2.65 us
  transfers between devices with their start and end apart: 8, of which 4 were waited for; matrix products, arithmetic and copies ran while one was open for 0% of the time, Pallas kernels for 56%

profile of v3, /device:TPU:0, one launch (start us, length us, event | category | flops | bytes accessed | tf_op | source)
XLA Modules:
  0.0 59.3 jit_solution(10079908836911987108)
XLA Ops:
  0.6 1.7 %table.1 = (f32[128,128]{1,0:T(8,128)}, s32[1,2048]{1,0:T(1,128)}) custom-call(f32[9,3,512]{2,1,0:T(4,128)} %bitcast.13, f32[9,3,512]{2,1,0:T(4,128)} %bitcast.14, s32[1,2048]{1,0:T(1,128)} %bitcast.22, s32[1,2048]{1,0:T(1,128)} %bitcast.19), custom_call_target="tpu_custom_call" | custom-call | tf_op jit(solution)/shard_map/table/pallas_call | solution.py:442
  2.3 3.0 %collective-permute-start.2 = (f32[128,128]{1,0:T(8,128)}, f32[128,128]{1,0:T(8,128)S(1)}, u32[]{:S(2)}, u32[]{:S(2)}) collective-permute-start(f32[128,128]{1,0:T(8,128)} %get-tuple-element.22), channel_id=1, source_target_pairs={{24,0},{0,8},{8,16},{16,24},{25,1},{1,9},{9,17},{17,25},{26,2},{2,... | collective-permute-start | bytes 196616 | tf_op jit(solution)/shard_map/ppermute | solution.py:381
  5.3 2.6 %collective-permute-start.1 = (f32[128,128]{1,0:T(8,128)}, f32[128,128]{1,0:T(8,128)S(1)}, u32[]{:S(2)}, u32[]{:S(2)}) collective-permute-start(f32[128,128]{1,0:T(8,128)} %get-tuple-element.22), channel_id=1, source_target_pairs={{16,0},{24,8},{0,16},{8,24},{17,1},{25,9},{1,17},{9,25},{18,2},{26... | collective-permute-start | bytes 196616 | tf_op jit(solution)/shard_map/ppermute | solution.py:381
  7.9 1.3 %collective-permute-start = (f32[128,128]{1,0:T(8,128)}, f32[128,128]{1,0:T(8,128)S(1)}, u32[]{:S(2)}, u32[]{:S(2)}) collective-permute-start(f32[128,128]{1,0:T(8,128)} %get-tuple-element.22), channel_id=1, source_target_pairs={{8,0},{16,8},{24,16},{0,24},{9,1},{17,9},{25,17},{1,25},{10,2},{18... | collective-permute-start | bytes 196616 | tf_op jit(solution)/shard_map/ppermute | solution.py:381
  9.3 0.0 copy-start.2
  9.3 14.2 %terms.1 = (f32[81,2048]{1,0:T(8,128)}, f32[56,2048]{1,0:T(8,128)S(1)}, f32[16,5,128,128]{3,2,1,0:T(8,128)}) custom-call(f32[4096,128]{1,0:T(8,128)} %bitcast.11, f32[4096,128]{1,0:T(8,128)} %bitcast.12, f32[2048,128]{1,0:T(8,128)} %w_ref.1, s32[1,2048]{1,0:T(1,128)} %bitcast.24, s32[1,2048]{1,0:T(1,128)} %bitcast.20, f32[9,3,512]{2,1,0:T(4,128)} %bitcast.15, ...), custom_call_target="tpu_custom_call" | custom-call | flops 1000000000 | bytes 15000000 | tf_op jit(solution)/shard_map/terms/pallas_call | solution.py:466
  23.4 0.0 collective-permute-done.2
  23.4 0.0 collective-permute-done.1
  23.5 0.0 collective-permute-done
  23.5 0.0 copy-done.2
  23.5 2.5 %collective-permute-start.5 = (f32[512,128]{1,0:T(8,128)S(1)}, f32[512,128]{1,0:T(8,128)S(1)}, u32[]{:S(2)}, u32[]{:S(2)}) collective-permute-start(f32[512,128]{1,0:T(8,128)S(1)} %pad_maximum_fusion), channel_id=1, source_target_pairs={{6,0},{7,1},{4,2},{5,3},{2,4},{3,5},{0,6},{1,7},{14,8},{15,9},{12,... | collective-permute-start | bytes 786440 | tf_op jit(solution)/shard_map/ppermute | solution.py:389
  26.0 0.5 collective-permute-start.4
  26.5 0.5 collective-permute-start.3
  27.1 4.1 %slots.1 = f32[32,56,128]{2,1,0:T(8,128)} custom-call(s32[1,2048]{1,0:T(1,128)} %bitcast.23, f32[56,2048]{1,0:T(8,128)S(1)} %get-tuple-element.36.terms_ref), custom_call_target="tpu_custom_call" | custom-call | tf_op jit(solution)/shard_map/slots/pallas_call | solution.py:497
  31.1 0.0 copy-start
  31.1 0.0 copy-start.1
  31.1 2.9 %all-to-all-start = ((f32[32,56,128]{2,1,0:T(8,128)}), f32[32,56,128]{2,1,0:T(8,128)S(1)}, u32[]{:S(2)}, u32[]{:S(2)}) async-start(f32[32,56,128]{2,1,0:T(8,128)} %slots.1), calls=%async_computation | async-start | bytes 1835008 | tf_op jit(solution)/shard_map/all_to_all | solution.py:506
  34.1 0.0 collective-permute-done.5
  34.1 3.3 %collective-permute-done.4 = f32[512,128]{1,0:T(8,128)S(1)} collective-permute-done((f32[512,128]{1,0:T(8,128)S(1)}, f32[512,128]{1,0:T(8,128)S(1)}, u32[]{:S(2)}, u32[]{:S(2)}) %collective-permute-start.4) | collective-permute-done | bytes 262176 | tf_op jit(solution)/shard_map/ppermute | solution.py:389
  37.4 1.0 %collective-permute-done.3 = f32[512,128]{1,0:T(8,128)S(1)} collective-permute-done((f32[512,128]{1,0:T(8,128)S(1)}, f32[512,128]{1,0:T(8,128)S(1)}, u32[]{:S(2)}, u32[]{:S(2)}) %collective-permute-start.3) | collective-permute-done | bytes 262176 | tf_op jit(solution)/shard_map/ppermute | solution.py:389
  38.5 0.1 collective-permute-start.6
  38.5 2.6 %collective-permute-done.6.far_ref = f32[2048,128]{1,0:T(8,128)S(1)} collective-permute-done((f32[2048,128]{1,0:T(8,128)S(1)}, f32[2048,128]{1,0:T(8,128)S(1)}, u32[]{:S(2)}, u32[]{:S(2)}) %collective-permute-start.6) | collective-permute-done | bytes 1048608 | tf_op jit(solution)/shard_map/ppermute | solution.py:394
  41.2 0.0 copy-done
  41.2 0.0 copy-done.1
  41.2 15.0 %gap.1 = (f32[9,512]{1,0:T(8,128)}, f32[81,512]{1,0:T(8,128)}) custom-call(s32[1,2048]{1,0:T(1,128)S(1)} %copy-done.1, f32[16,5,128,128]{3,2,1,0:T(8,128)} %get-tuple-element.28.planes_ref, s32[1,2048]{1,0:T(1,128)} %bitcast.25, s32[1,2048]{1,0:T(1,128)} %bitcast.21, f32[9,3,512]{2,1,0:T(4,128)} %bitcast.16, f32[9,3,512]{2,1,0:T(4,128)} %bitcast.17, ...), custom_call_target="tpu_custom_call" | custom-call | flops 2000000000 | bytes 60000000 | tf_op jit(solution)/shard_map/gap/pallas_call | solution.py:514
  56.2 1.3 %all-to-all-done.in_ref = f32[32,56,128]{2,1,0:T(8,128)S(1)} async-done(((f32[32,56,128]{2,1,0:T(8,128)}), f32[32,56,128]{2,1,0:T(8,128)S(1)}, u32[]{:S(2)}, u32[]{:S(2)}) %all-to-all-start) | async-done | bytes 917536 | tf_op jit(solution)/shard_map/all_to_all | solution.py:506
  57.5 1.8 %owner.1 = (f32[27,512]{1,0:T(8,128)}, f32[81,512]{1,0:T(8,128)}) custom-call(f32[32,56,128]{2,1,0:T(8,128)S(1)} %all-to-all-done.in_ref, bf16[81,32]{1,0:T(8,128)(2,1)S(1)} %copy-done), custom_call_target="tpu_custom_call" | custom-call | tf_op jit(solution)/shard_map/owner/pallas_call | solution.py:539
  (5 shorter events, 0.1 us)
Async XLA Ops:
  2.3 21.1 %collective-permute-start.2 = (f32[128,128]{1,0:T(8,128)}, f32[128,128]{1,0:T(8,128)S(1)}, u32[]{:S(2)}, u32[]{:S(2)}) collective-permute-start(f32[128,128]{1,0:T(8,128)} %get-tuple-element.22), channel_id=1, source_target_pairs={{24,0},{0,8},{8,16},{16,24},{25,1},{1,9},{9,17},{17,25},{26,2},{2,... | collective-permute-start | bytes 196616 | tf_op jit(solution)/shard_map/ppermute | solution.py:381
  5.3 18.1 %collective-permute-start.1 = (f32[128,128]{1,0:T(8,128)}, f32[128,128]{1,0:T(8,128)S(1)}, u32[]{:S(2)}, u32[]{:S(2)}) collective-permute-start(f32[128,128]{1,0:T(8,128)} %get-tuple-element.22), channel_id=1, source_target_pairs={{16,0},{24,8},{0,16},{8,24},{17,1},{25,9},{1,17},{9,25},{18,2},{26... | collective-permute-start | bytes 196616 | tf_op jit(solution)/shard_map/ppermute | solution.py:381
  7.9 15.5 %collective-permute-start = (f32[128,128]{1,0:T(8,128)}, f32[128,128]{1,0:T(8,128)S(1)}, u32[]{:S(2)}, u32[]{:S(2)}) collective-permute-start(f32[128,128]{1,0:T(8,128)} %get-tuple-element.22), channel_id=1, source_target_pairs={{8,0},{16,8},{24,16},{0,24},{9,1},{17,9},{25,17},{1,25},{10,2},{18... | collective-permute-start | bytes 196616 | tf_op jit(solution)/shard_map/ppermute | solution.py:381
  9.3 14.2 %copy-start.2 = (f32[128,128]{1,0:T(8,128)S(1)}, f32[128,128]{1,0:T(8,128)}, u32[]{:S(2)}) copy-start(f32[128,128]{1,0:T(8,128)} %get-tuple-element.22) | copy-start | bytes 196612
  23.5 10.6 %collective-permute-start.5 = (f32[512,128]{1,0:T(8,128)S(1)}, f32[512,128]{1,0:T(8,128)S(1)}, u32[]{:S(2)}, u32[]{:S(2)}) collective-permute-start(f32[512,128]{1,0:T(8,128)S(1)} %pad_maximum_fusion), channel_id=1, source_target_pairs={{6,0},{7,1},{4,2},{5,3},{2,4},{3,5},{0,6},{1,7},{14,8},{15,9},{12,... | collective-permute-start | bytes 786440 | tf_op jit(solution)/shard_map/ppermute | solution.py:389
  26.0 11.4 %collective-permute-start.4 = (f32[512,128]{1,0:T(8,128)S(1)}, f32[512,128]{1,0:T(8,128)S(1)}, u32[]{:S(2)}, u32[]{:S(2)}) collective-permute-start(f32[512,128]{1,0:T(8,128)S(1)} %pad_maximum_fusion), channel_id=1, source_target_pairs={{4,0},{5,1},{6,2},{7,3},{0,4},{1,5},{2,6},{3,7},{12,8},{13,9},{14,... | collective-permute-start | bytes 786440 | tf_op jit(solution)/shard_map/ppermute | solution.py:389
  26.5 11.8 %collective-permute-start.3 = (f32[512,128]{1,0:T(8,128)S(1)}, f32[512,128]{1,0:T(8,128)S(1)}, u32[]{:S(2)}, u32[]{:S(2)}) collective-permute-start(f32[512,128]{1,0:T(8,128)S(1)} %pad_maximum_fusion), channel_id=1, source_target_pairs={{2,0},{3,1},{0,2},{1,3},{6,4},{7,5},{4,6},{5,7},{10,8},{11,9},{8,1... | collective-permute-start | bytes 786440 | tf_op jit(solution)/shard_map/ppermute | solution.py:389
  31.1 10.1 %copy-start = (bf16[81,32]{1,0:T(8,128)(2,1)S(1)}, bf16[81,32]{1,0:T(8,128)(2,1)}, u32[]{:S(2)}) copy-start(bf16[81,32]{1,0:T(8,128)(2,1)} %constant.5.clone.expand_ref) | copy-start | bytes 15556
  31.1 10.1 %copy-start.1 = (s32[1,2048]{1,0:T(1,128)S(1)}, s32[1,2048]{1,0:T(1,128)}, u32[]{:S(2)}) copy-start(s32[1,2048]{1,0:T(1,128)} %get-tuple-element.27.row_ref) | copy-start | bytes 24580
  31.1 26.4 %all-to-all-start = ((f32[32,56,128]{2,1,0:T(8,128)}), f32[32,56,128]{2,1,0:T(8,128)S(1)}, u32[]{:S(2)}, u32[]{:S(2)}) async-start(f32[32,56,128]{2,1,0:T(8,128)} %slots.1), calls=%async_computation | async-start | bytes 1835008 | tf_op jit(solution)/shard_map/all_to_all | solution.py:506
  38.5 2.7 %collective-permute-start.6 = (f32[2048,128]{1,0:T(8,128)S(1)}, f32[2048,128]{1,0:T(8,128)S(1)}, u32[]{:S(2)}, u32[]{:S(2)}) collective-permute-start(f32[2048,128]{1,0:T(8,128)S(1)} %constant_dynamic-update-slice_fusion.near_ref), channel_id=1, source_target_pairs={{1,0},{0,1},{3,2},{2,3},{5,4},{4,5},{7,6},{6,7},{9,8},{8,9},{11,10... | collective-permute-start | bytes 3145736 | tf_op jit(solution)/shard_map/ppermute | solution.py:394

commit v4 on v3

--- a/solution.py
+++ b/solution.py
@@ -10,7 +10,7 @@
 
 AXES = ("patch", "seg")
 BLOCK = 128
-SUB = 2
+SUB = 4
 GAP_FLOPS = 2 * 10**9
 GAP_BYTES = 60 * 10**6
 UNROLL = (16, 16, 16)
@@ -26,7 +26,7 @@
     table = np.zeros((88, 96), np.float32)
     for at, column in enumerate(np.einsum("ac,bd->cdab", nodes, nodes).reshape(81, 81)):
         table[:81, 32 * (at // 27) + at % 27] = column
-    return table
+    return np.concatenate([table, table], axis=1)
 
 
 def power_products():
@@ -172,7 +172,7 @@
     for sub in range(SUB):
         crossed_sums(sub, planes_ref, shape_ref, c_ref, terms_ref)
     moments = c_ref[...]
-    coupling = expanded(couple_ref[...], moments)
+    coupling = dot(couple_ref[...], stack2(moments))
     coupling_ref[...] = coupling[0:81]
     for a in range(9):
         block_ref[a, 0:9, :] = coupling[9 * a : 9 * a + 9]
@@ -482,7 +482,7 @@
                 pltpu.VMEM((64, segments), BF16),
             ],
             input_output_aliases={7 + i: i for i in range(len(previous))},
-            compiler_params=vmem(16),
+            compiler_params=vmem(28),
             cost_estimate=pl.CostEstimate(flops=10**9, transcendentals=0, bytes_accessed=15 * 10**6),
             name="terms",
         )(qs, qm, qw, sl, ml, multipliers, couple, *previous)
@@ -498,7 +498,7 @@
         functools.partial(slots_kernel, devices=devices, cap=cap),
         out_shape=jax.ShapeDtypeStruct(shape, F32),
         scratch_shapes=[pltpu.VMEM((112 * devices * cap // 256, pairs), BF16)],
-        compiler_params=vmem(24),
+        compiler_params=vmem(30),
         name="slots",
     )(owner, terms)
     if cap != 128:
@@ -531,7 +531,7 @@
             pltpu.VMEM((segments, pairs), BF16),
             pltpu.SemaphoreType.DMA((2,)),
         ],
-        compiler_params=vmem(24),
+        compiler_params=vmem(30),
         cost_estimate=pl.CostEstimate(flops=GAP_FLOPS, transcendentals=0, bytes_accessed=GAP_BYTES),
         name="gap",
     )(rows, quads, sl, ml, slave_coords, slave_disp, slave_normals, expand, plane, other)
@@ -539,7 +539,7 @@
     force, master_mass = pl.pallas_call(
         owner_kernel,
         out_shape=[jax.ShapeDtypeStruct((27, segments), F32), jax.ShapeDtypeStruct((81, segments), F32)],
-        compiler_params=vmem(16),
+        compiler_params=vmem(28),
         name="owner",
     )(incoming, expand)
     return coupling, weighted_gap, slave_mass, force, master_mass

time: 59.7 us -> 58.2 us (0.975)
  Pallas kernels: 36.7 us -> 35.1 us
    pallas_call x1, Pallas kernels: 14.2 us -> 12.7 us  [terms_call(): pl.pallas_call(terms_kernel, grid=(last - first,), in_specs=[quad, quad,...]
  transfers between devices with their start and end apart: 8 -> 8, of which waited for: 4 -> 4; matrix products, arithmetic and copies ran while one was open for 0% -> 0% of each run, Pallas kernels for 56% -> 55%
where the time goes in v4:
time: 58.2 us; the launch traced here: 57.8 us
  Pallas kernels  35.1 us (60%)
  starting transfers between devices  13.5 us (23%)
  waiting for transfers between devices  8.32 us (14%)
  between operations  0.73 us (1%)
    pallas_call x1, Pallas kernels, shards(): pl.pallas_call(gap_kernel, grid=(steps,), in_specs=[pl.BlockSpec(memory_s...  14.9 us
    pallas_call x1, Pallas kernels, terms_call(): pl.pallas_call(terms_kernel, grid=(last - first,), in_specs=[quad, quad,...  12.7 us
    ppermute x3, starting transfers between devices, from_patches(): lax.ppermute(block, 'patch', [((i + d) % patches, i) for i in range(patch...  6.96 us
    ppermute x3, waiting for transfers between devices, from_chips(): lax.ppermute(column, 'seg', [(i ^ 2 * d, i) for i in range(segs)])  4.29 us
    pallas_call x1, Pallas kernels, shards(): pl.pallas_call(functools.partial(slots_kernel, devices=devices, cap=cap),...  4.06 us
    ppermute x3, starting transfers between devices, from_chips(): lax.ppermute(column, 'seg', [(i ^ 2 * d, i) for i in range(segs)])  3.55 us
    all_to_all x1, starting transfers between devices, shards(): lax.all_to_all(outgoing, AXES, split_axis=0, concat_axis=0, tiled=True)  2.93 us
    ppermute x1, waiting for transfers between devices, from_core(): lax.ppermute(plane, 'seg', [(i ^ 1, i) for i in range(lax.axis_size('seg'...  2.65 us
  transfers between devices with their start and end apart: 8, of which 4 were waited for; matrix products, arithmetic and copies ran while one was open for 0% of the time, Pallas kernels for 55%

profile of v4, /device:TPU:0, one launch (start us, length us, event | category | flops | bytes accessed | tf_op | source)
XLA Modules:
  0.0 57.8 jit_solution(16823820131172042823)
XLA Ops:
  0.6 1.7 %table.1 = (f32[128,128]{1,0:T(8,128)}, s32[1,2048]{1,0:T(1,128)}) custom-call(f32[9,3,512]{2,1,0:T(4,128)} %bitcast.13, f32[9,3,512]{2,1,0:T(4,128)} %bitcast.14, s32[1,2048]{1,0:T(1,128)} %bitcast.22, s32[1,2048]{1,0:T(1,128)} %bitcast.19), custom_call_target="tpu_custom_call" | custom-call | tf_op jit(solution)/shard_map/table/pallas_call | solution.py:442
  2.3 3.0 %collective-permute-start.2 = (f32[128,128]{1,0:T(8,128)}, f32[128,128]{1,0:T(8,128)S(1)}, u32[]{:S(2)}, u32[]{:S(2)}) collective-permute-start(f32[128,128]{1,0:T(8,128)} %get-tuple-element.22), channel_id=1, source_target_pairs={{24,0},{0,8},{8,16},{16,24},{25,1},{1,9},{9,17},{17,25},{26,2},{2,... | collective-permute-start | bytes 196616 | tf_op jit(solution)/shard_map/ppermute | solution.py:381
  5.3 2.6 %collective-permute-start.1 = (f32[128,128]{1,0:T(8,128)}, f32[128,128]{1,0:T(8,128)S(1)}, u32[]{:S(2)}, u32[]{:S(2)}) collective-permute-start(f32[128,128]{1,0:T(8,128)} %get-tuple-element.22), channel_id=1, source_target_pairs={{16,0},{24,8},{0,16},{8,24},{17,1},{25,9},{1,17},{9,25},{18,2},{26... | collective-permute-start | bytes 196616 | tf_op jit(solution)/shard_map/ppermute | solution.py:381
  7.9 1.3 %collective-permute-start = (f32[128,128]{1,0:T(8,128)}, f32[128,128]{1,0:T(8,128)S(1)}, u32[]{:S(2)}, u32[]{:S(2)}) collective-permute-start(f32[128,128]{1,0:T(8,128)} %get-tuple-element.22), channel_id=1, source_target_pairs={{8,0},{16,8},{24,16},{0,24},{9,1},{17,9},{25,17},{1,25},{10,2},{18... | collective-permute-start | bytes 196616 | tf_op jit(solution)/shard_map/ppermute | solution.py:381
  9.3 0.0 copy-start.2
  9.3 12.7 %terms.1 = (f32[81,2048]{1,0:T(8,128)}, f32[56,2048]{1,0:T(8,128)S(1)}, f32[16,5,128,128]{3,2,1,0:T(8,128)}) custom-call(f32[4096,128]{1,0:T(8,128)} %bitcast.11, f32[4096,128]{1,0:T(8,128)} %bitcast.12, f32[2048,128]{1,0:T(8,128)} %w_ref.1, s32[1,2048]{1,0:T(1,128)} %bitcast.24, s32[1,2048]{1,0:T(1,128)} %bitcast.20, f32[9,3,512]{2,1,0:T(4,128)} %bitcast.15, ...), custom_call_target="tpu_custom_call" | custom-call | flops 1000000000 | bytes 15000000 | tf_op jit(solution)/shard_map/terms/pallas_call | solution.py:466
  21.9 0.0 collective-permute-done.2
  21.9 0.0 collective-permute-done.1
  21.9 0.0 collective-permute-done
  22.0 0.0 copy-done.2
  22.0 2.5 %collective-permute-start.5 = (f32[512,128]{1,0:T(8,128)S(1)}, f32[512,128]{1,0:T(8,128)S(1)}, u32[]{:S(2)}, u32[]{:S(2)}) collective-permute-start(f32[512,128]{1,0:T(8,128)S(1)} %pad_maximum_fusion), channel_id=1, source_target_pairs={{6,0},{7,1},{4,2},{5,3},{2,4},{3,5},{0,6},{1,7},{14,8},{15,9},{12,... | collective-permute-start | bytes 786440 | tf_op jit(solution)/shard_map/ppermute | solution.py:389
  24.5 0.5 collective-permute-start.4
  25.0 0.5 collective-permute-start.3
  25.6 4.1 %slots.1 = f32[32,56,128]{2,1,0:T(8,128)} custom-call(s32[1,2048]{1,0:T(1,128)} %bitcast.23, f32[56,2048]{1,0:T(8,128)S(1)} %get-tuple-element.36.terms_ref), custom_call_target="tpu_custom_call" | custom-call | tf_op jit(solution)/shard_map/slots/pallas_call | solution.py:497
  29.6 0.0 copy-start
  29.6 0.0 copy-start.1
  29.6 2.9 %all-to-all-start = ((f32[32,56,128]{2,1,0:T(8,128)}), f32[32,56,128]{2,1,0:T(8,128)S(1)}, u32[]{:S(2)}, u32[]{:S(2)}) async-start(f32[32,56,128]{2,1,0:T(8,128)} %slots.1), calls=%async_computation | async-start | bytes 1835008 | tf_op jit(solution)/shard_map/all_to_all | solution.py:506
  32.6 0.0 collective-permute-done.5
  32.6 3.3 %collective-permute-done.4 = f32[512,128]{1,0:T(8,128)S(1)} collective-permute-done((f32[512,128]{1,0:T(8,128)S(1)}, f32[512,128]{1,0:T(8,128)S(1)}, u32[]{:S(2)}, u32[]{:S(2)}) %collective-permute-start.4) | collective-permute-done | bytes 262176 | tf_op jit(solution)/shard_map/ppermute | solution.py:389
  35.9 1.0 %collective-permute-done.3 = f32[512,128]{1,0:T(8,128)S(1)} collective-permute-done((f32[512,128]{1,0:T(8,128)S(1)}, f32[512,128]{1,0:T(8,128)S(1)}, u32[]{:S(2)}, u32[]{:S(2)}) %collective-permute-start.3) | collective-permute-done | bytes 262176 | tf_op jit(solution)/shard_map/ppermute | solution.py:389
  37.0 0.1 collective-permute-start.6
  37.0 2.6 %collective-permute-done.6.far_ref = f32[2048,128]{1,0:T(8,128)S(1)} collective-permute-done((f32[2048,128]{1,0:T(8,128)S(1)}, f32[2048,128]{1,0:T(8,128)S(1)}, u32[]{:S(2)}, u32[]{:S(2)}) %collective-permute-start.6) | collective-permute-done | bytes 1048608 | tf_op jit(solution)/shard_map/ppermute | solution.py:394
  39.7 0.0 copy-done
  39.7 0.0 copy-done.1
  39.7 14.9 %gap.1 = (f32[9,512]{1,0:T(8,128)}, f32[81,512]{1,0:T(8,128)}) custom-call(s32[1,2048]{1,0:T(1,128)S(1)} %copy-done.1, f32[16,5,128,128]{3,2,1,0:T(8,128)} %get-tuple-element.28.planes_ref, s32[1,2048]{1,0:T(1,128)} %bitcast.25, s32[1,2048]{1,0:T(1,128)} %bitcast.21, f32[9,3,512]{2,1,0:T(4,128)} %bitcast.16, f32[9,3,512]{2,1,0:T(4,128)} %bitcast.17, ...), custom_call_target="tpu_custom_call" | custom-call | flops 2000000000 | bytes 60000000 | tf_op jit(solution)/shard_map/gap/pallas_call | solution.py:514
  54.6 1.4 %all-to-all-done.in_ref = f32[32,56,128]{2,1,0:T(8,128)S(1)} async-done(((f32[32,56,128]{2,1,0:T(8,128)}), f32[32,56,128]{2,1,0:T(8,128)S(1)}, u32[]{:S(2)}, u32[]{:S(2)}) %all-to-all-start) | async-done | bytes 917536 | tf_op jit(solution)/shard_map/all_to_all | solution.py:506
  56.0 1.8 %owner.1 = (f32[27,512]{1,0:T(8,128)}, f32[81,512]{1,0:T(8,128)}) custom-call(f32[32,56,128]{2,1,0:T(8,128)S(1)} %all-to-all-done.in_ref, bf16[81,32]{1,0:T(8,128)(2,1)S(1)} %copy-done), custom_call_target="tpu_custom_call" | custom-call | tf_op jit(solution)/shard_map/owner/pallas_call | solution.py:539
  (5 shorter events, 0.1 us)
Async XLA Ops:
  2.3 19.6 %collective-permute-start.2 = (f32[128,128]{1,0:T(8,128)}, f32[128,128]{1,0:T(8,128)S(1)}, u32[]{:S(2)}, u32[]{:S(2)}) collective-permute-start(f32[128,128]{1,0:T(8,128)} %get-tuple-element.22), channel_id=1, source_target_pairs={{24,0},{0,8},{8,16},{16,24},{25,1},{1,9},{9,17},{17,25},{26,2},{2,... | collective-permute-start | bytes 196616 | tf_op jit(solution)/shard_map/ppermute | solution.py:381
  5.3 16.6 %collective-permute-start.1 = (f32[128,128]{1,0:T(8,128)}, f32[128,128]{1,0:T(8,128)S(1)}, u32[]{:S(2)}, u32[]{:S(2)}) collective-permute-start(f32[128,128]{1,0:T(8,128)} %get-tuple-element.22), channel_id=1, source_target_pairs={{16,0},{24,8},{0,16},{8,24},{17,1},{25,9},{1,17},{9,25},{18,2},{26... | collective-permute-start | bytes 196616 | tf_op jit(solution)/shard_map/ppermute | solution.py:381
  7.9 14.0 %collective-permute-start = (f32[128,128]{1,0:T(8,128)}, f32[128,128]{1,0:T(8,128)S(1)}, u32[]{:S(2)}, u32[]{:S(2)}) collective-permute-start(f32[128,128]{1,0:T(8,128)} %get-tuple-element.22), channel_id=1, source_target_pairs={{8,0},{16,8},{24,16},{0,24},{9,1},{17,9},{25,17},{1,25},{10,2},{18... | collective-permute-start | bytes 196616 | tf_op jit(solution)/shard_map/ppermute | solution.py:381
  9.3 12.7 %copy-start.2 = (f32[128,128]{1,0:T(8,128)S(1)}, f32[128,128]{1,0:T(8,128)}, u32[]{:S(2)}) copy-start(f32[128,128]{1,0:T(8,128)} %get-tuple-element.22) | copy-start | bytes 196612
  22.0 10.6 %collective-permute-start.5 = (f32[512,128]{1,0:T(8,128)S(1)}, f32[512,128]{1,0:T(8,128)S(1)}, u32[]{:S(2)}, u32[]{:S(2)}) collective-permute-start(f32[512,128]{1,0:T(8,128)S(1)} %pad_maximum_fusion), channel_id=1, source_target_pairs={{6,0},{7,1},{4,2},{5,3},{2,4},{3,5},{0,6},{1,7},{14,8},{15,9},{12,... | collective-permute-start | bytes 786440 | tf_op jit(solution)/shard_map/ppermute | solution.py:389
  24.5 11.4 %collective-permute-start.4 = (f32[512,128]{1,0:T(8,128)S(1)}, f32[512,128]{1,0:T(8,128)S(1)}, u32[]{:S(2)}, u32[]{:S(2)}) collective-permute-start(f32[512,128]{1,0:T(8,128)S(1)} %pad_maximum_fusion), channel_id=1, source_target_pairs={{4,0},{5,1},{6,2},{7,3},{0,4},{1,5},{2,6},{3,7},{12,8},{13,9},{14,... | collective-permute-start | bytes 786440 | tf_op jit(solution)/shard_map/ppermute | solution.py:389
  25.0 11.8 %collective-permute-start.3 = (f32[512,128]{1,0:T(8,128)S(1)}, f32[512,128]{1,0:T(8,128)S(1)}, u32[]{:S(2)}, u32[]{:S(2)}) collective-permute-start(f32[512,128]{1,0:T(8,128)S(1)} %pad_maximum_fusion), channel_id=1, source_target_pairs={{2,0},{3,1},{0,2},{1,3},{6,4},{7,5},{4,6},{5,7},{10,8},{11,9},{8,1... | collective-permute-start | bytes 786440 | tf_op jit(solution)/shard_map/ppermute | solution.py:389
  29.6 10.1 %copy-start = (bf16[81,32]{1,0:T(8,128)(2,1)S(1)}, bf16[81,32]{1,0:T(8,128)(2,1)}, u32[]{:S(2)}) copy-start(bf16[81,32]{1,0:T(8,128)(2,1)} %constant.5.clone.expand_ref) | copy-start | bytes 15556
  29.6 10.1 %copy-start.1 = (s32[1,2048]{1,0:T(1,128)S(1)}, s32[1,2048]{1,0:T(1,128)}, u32[]{:S(2)}) copy-start(s32[1,2048]{1,0:T(1,128)} %get-tuple-element.27.row_ref) | copy-start | bytes 24580
  29.6 26.4 %all-to-all-start = ((f32[32,56,128]{2,1,0:T(8,128)}), f32[32,56,128]{2,1,0:T(8,128)S(1)}, u32[]{:S(2)}, u32[]{:S(2)}) async-start(f32[32,56,128]{2,1,0:T(8,128)} %slots.1), calls=%async_computation | async-start | bytes 1835008 | tf_op jit(solution)/shard_map/all_to_all | solution.py:506
  37.0 2.7 %collective-permute-start.6 = (f32[2048,128]{1,0:T(8,128)S(1)}, f32[2048,128]{1,0:T(8,128)S(1)}, u32[]{:S(2)}, u32[]{:S(2)}) collective-permute-start(f32[2048,128]{1,0:T(8,128)S(1)} %constant_dynamic-update-slice_fusion.near_ref), channel_id=1, source_target_pairs={{1,0},{0,1},{3,2},{2,3},{5,4},{4,5},{7,6},{6,7},{9,8},{8,9},{11,10... | collective-permute-start | bytes 3145736 | tf_op jit(solution)/shard_map/ppermute | solution.py:394

commit v5 on v4

--- a/solution.py
+++ b/solution.py
@@ -10,7 +10,7 @@
 
 AXES = ("patch", "seg")
 BLOCK = 128
-SUB = 4
+SUB = 8
 GAP_FLOPS = 2 * 10**9
 GAP_BYTES = 60 * 10**6
 UNROLL = (16, 16, 16)
@@ -482,7 +482,7 @@
                 pltpu.VMEM((64, segments), BF16),
             ],
             input_output_aliases={7 + i: i for i in range(len(previous))},
-            compiler_params=vmem(28),
+            compiler_params=vmem(48),
             cost_estimate=pl.CostEstimate(flops=10**9, transcendentals=0, bytes_accessed=15 * 10**6),
             name="terms",
         )(qs, qm, qw, sl, ml, multipliers, couple, *previous)
@@ -498,7 +498,7 @@
         functools.partial(slots_kernel, devices=devices, cap=cap),
         out_shape=jax.ShapeDtypeStruct(shape, F32),
         scratch_shapes=[pltpu.VMEM((112 * devices * cap // 256, pairs), BF16)],
-        compiler_params=vmem(30),
+        compiler_params=vmem(48),
         name="slots",
     )(owner, terms)
     if cap != 128:
@@ -531,7 +531,7 @@
             pltpu.VMEM((segments, pairs), BF16),
             pltpu.SemaphoreType.DMA((2,)),
         ],
-        compiler_params=vmem(30),
+        compiler_params=vmem(48),
         cost_estimate=pl.CostEstimate(flops=GAP_FLOPS, transcendentals=0, bytes_accessed=GAP_BYTES),
         name="gap",
     )(rows, quads, sl, ml, slave_coords, slave_disp, slave_normals, expand, plane, other)
@@ -539,7 +539,7 @@
     force, master_mass = pl.pallas_call(
         owner_kernel,
         out_shape=[jax.ShapeDtypeStruct((27, segments), F32), jax.ShapeDtypeStruct((81, segments), F32)],
-        compiler_params=vmem(28),
+        compiler_params=vmem(48),
         name="owner",
     )(incoming, expand)
     return coupling, weighted_gap, slave_mass, force, master_mass

time: 58.2 us -> 58.7 us (level)
  Pallas kernels: 35.1 us -> 36.1 us
    pallas_call x1, Pallas kernels: 12.7 us -> 13.3 us  [terms_call(): pl.pallas_call(terms_kernel, grid=(last - first,), in_specs=[quad, quad,...]
  transfers between devices with their start and end apart: 8 -> 8, of which waited for: 4 -> 4; matrix products, arithmetic and copies ran while one was open for 0% -> 0% of each run, Pallas kernels for 55% -> 56%
where the time goes in v5:
time: 58.7 us; the launch traced here: 58.4 us
  Pallas kernels  36.1 us (61%)
  starting transfers between devices  13.7 us (23%)
  waiting for transfers between devices  7.76 us (13%)
  between operations  0.73 us (1%)
    pallas_call x1, Pallas kernels, shards(): pl.pallas_call(gap_kernel, grid=(steps,), in_specs=[pl.BlockSpec(memory_s...  15.3 us
    pallas_call x1, Pallas kernels, terms_call(): pl.pallas_call(terms_kernel, grid=(last - first,), in_specs=[quad, quad,...  13.3 us
    ppermute x3, starting transfers between devices, from_patches(): lax.ppermute(block, 'patch', [((i + d) % patches, i) for i in range(patch...  6.96 us
    ppermute x3, waiting for transfers between devices, from_chips(): lax.ppermute(column, 'seg', [(i ^ 2 * d, i) for i in range(segs)])  4.11 us
    pallas_call x1, Pallas kernels, shards(): pl.pallas_call(functools.partial(slots_kernel, devices=devices, cap=cap),...  4.06 us
    ppermute x3, starting transfers between devices, from_chips(): lax.ppermute(column, 'seg', [(i ^ 2 * d, i) for i in range(segs)])  3.55 us
    all_to_all x1, starting transfers between devices, shards(): lax.all_to_all(outgoing, AXES, split_axis=0, concat_axis=0, tiled=True)  3.11 us
    ppermute x1, waiting for transfers between devices, from_core(): lax.ppermute(plane, 'seg', [(i ^ 1, i) for i in range(lax.axis_size('seg'...  2.65 us
  transfers between devices with their start and end apart: 8, of which 4 were waited for; matrix products, arithmetic and copies ran while one was open for 0% of the time, Pallas kernels for 56%

profile of v5, /device:TPU:0, one launch (start us, length us, event | category | flops | bytes accessed | tf_op | source)
XLA Modules:
  0.0 58.4 jit_solution(11832371312582447471)
XLA Ops:
  0.6 1.7 %table.1 = (f32[128,128]{1,0:T(8,128)}, s32[1,2048]{1,0:T(1,128)}) custom-call(f32[9,3,512]{2,1,0:T(4,128)} %bitcast.13, f32[9,3,512]{2,1,0:T(4,128)} %bitcast.14, s32[1,2048]{1,0:T(1,128)} %bitcast.22, s32[1,2048]{1,0:T(1,128)} %bitcast.19), custom_call_target="tpu_custom_call" | custom-call | tf_op jit(solution)/shard_map/table/pallas_call | solution.py:442
  2.3 3.0 %collective-permute-start.2 = (f32[128,128]{1,0:T(8,128)}, f32[128,128]{1,0:T(8,128)S(1)}, u32[]{:S(2)}, u32[]{:S(2)}) collective-permute-start(f32[128,128]{1,0:T(8,128)} %get-tuple-element.22), channel_id=1, source_target_pairs={{24,0},{0,8},{8,16},{16,24},{25,1},{1,9},{9,17},{17,25},{26,2},{2,... | collective-permute-start | bytes 196616 | tf_op jit(solution)/shard_map/ppermute | solution.py:381
  5.3 2.6 %collective-permute-start.1 = (f32[128,128]{1,0:T(8,128)}, f32[128,128]{1,0:T(8,128)S(1)}, u32[]{:S(2)}, u32[]{:S(2)}) collective-permute-start(f32[128,128]{1,0:T(8,128)} %get-tuple-element.22), channel_id=1, source_target_pairs={{16,0},{24,8},{0,16},{8,24},{17,1},{25,9},{1,17},{9,25},{18,2},{26... | collective-permute-start | bytes 196616 | tf_op jit(solution)/shard_map/ppermute | solution.py:381
  7.9 1.3 %collective-permute-start = (f32[128,128]{1,0:T(8,128)}, f32[128,128]{1,0:T(8,128)S(1)}, u32[]{:S(2)}, u32[]{:S(2)}) collective-permute-start(f32[128,128]{1,0:T(8,128)} %get-tuple-element.22), channel_id=1, source_target_pairs={{8,0},{16,8},{24,16},{0,24},{9,1},{17,9},{25,17},{1,25},{10,2},{18... | collective-permute-start | bytes 196616 | tf_op jit(solution)/shard_map/ppermute | solution.py:381
  9.3 0.0 copy-start.2
  9.3 13.3 %terms.1 = (f32[81,2048]{1,0:T(8,128)}, f32[56,2048]{1,0:T(8,128)S(1)}, f32[16,5,128,128]{3,2,1,0:T(8,128)}) custom-call(f32[4096,128]{1,0:T(8,128)} %bitcast.11, f32[4096,128]{1,0:T(8,128)} %bitcast.12, f32[2048,128]{1,0:T(8,128)} %w_ref.1, s32[1,2048]{1,0:T(1,128)} %bitcast.24, s32[1,2048]{1,0:T(1,128)} %bitcast.20, f32[9,3,512]{2,1,0:T(4,128)} %bitcast.15, ...), custom_call_target="tpu_custom_call" | custom-call | flops 1000000000 | bytes 15000000 | tf_op jit(solution)/shard_map/terms/pallas_call | solution.py:466
  22.5 0.0 collective-permute-done.2
  22.5 0.0 collective-permute-done.1
  22.6 0.0 collective-permute-done
  22.6 0.0 copy-done.2
  22.6 2.5 %collective-permute-start.5 = (f32[512,128]{1,0:T(8,128)S(1)}, f32[512,128]{1,0:T(8,128)S(1)}, u32[]{:S(2)}, u32[]{:S(2)}) collective-permute-start(f32[512,128]{1,0:T(8,128)S(1)} %pad_maximum_fusion), channel_id=1, source_target_pairs={{6,0},{7,1},{4,2},{5,3},{2,4},{3,5},{0,6},{1,7},{14,8},{15,9},{12,... | collective-permute-start | bytes 786440 | tf_op jit(solution)/shard_map/ppermute | solution.py:389
  25.1 0.5 collective-permute-start.4
  25.6 0.5 collective-permute-start.3
  26.2 4.1 %slots.1 = f32[32,56,128]{2,1,0:T(8,128)} custom-call(s32[1,2048]{1,0:T(1,128)} %bitcast.23, f32[56,2048]{1,0:T(8,128)S(1)} %get-tuple-element.36.terms_ref), custom_call_target="tpu_custom_call" | custom-call | tf_op jit(solution)/shard_map/slots/pallas_call | solution.py:497
  30.2 0.0 copy-start
  30.2 0.0 copy-start.1
  30.2 3.1 %all-to-all-start = ((f32[32,56,128]{2,1,0:T(8,128)}), f32[32,56,128]{2,1,0:T(8,128)S(1)}, u32[]{:S(2)}, u32[]{:S(2)}) async-start(f32[32,56,128]{2,1,0:T(8,128)} %slots.1), calls=%async_computation | async-start | bytes 1835008 | tf_op jit(solution)/shard_map/all_to_all | solution.py:506
  33.3 0.0 collective-permute-done.5
  33.3 3.1 %collective-permute-done.4 = f32[512,128]{1,0:T(8,128)S(1)} collective-permute-done((f32[512,128]{1,0:T(8,128)S(1)}, f32[512,128]{1,0:T(8,128)S(1)}, u32[]{:S(2)}, u32[]{:S(2)}) %collective-permute-start.4) | collective-permute-done | bytes 262176 | tf_op jit(solution)/shard_map/ppermute | solution.py:389
  36.5 1.0 %collective-permute-done.3 = f32[512,128]{1,0:T(8,128)S(1)} collective-permute-done((f32[512,128]{1,0:T(8,128)S(1)}, f32[512,128]{1,0:T(8,128)S(1)}, u32[]{:S(2)}, u32[]{:S(2)}) %collective-permute-start.3) | collective-permute-done | bytes 262176 | tf_op jit(solution)/shard_map/ppermute | solution.py:389
  37.6 0.1 collective-permute-start.6
  37.6 2.6 %collective-permute-done.6.far_ref = f32[2048,128]{1,0:T(8,128)S(1)} collective-permute-done((f32[2048,128]{1,0:T(8,128)S(1)}, f32[2048,128]{1,0:T(8,128)S(1)}, u32[]{:S(2)}, u32[]{:S(2)}) %collective-permute-start.6) | collective-permute-done | bytes 1048608 | tf_op jit(solution)/shard_map/ppermute | solution.py:394
  40.3 0.0 copy-done
  40.3 0.0 copy-done.1
  40.3 15.3 %gap.1 = (f32[9,512]{1,0:T(8,128)}, f32[81,512]{1,0:T(8,128)}) custom-call(s32[1,2048]{1,0:T(1,128)S(1)} %copy-done.1, f32[16,5,128,128]{3,2,1,0:T(8,128)} %get-tuple-element.28.planes_ref, s32[1,2048]{1,0:T(1,128)} %bitcast.25, s32[1,2048]{1,0:T(1,128)} %bitcast.21, f32[9,3,512]{2,1,0:T(4,128)} %bitcast.16, f32[9,3,512]{2,1,0:T(4,128)} %bitcast.17, ...), custom_call_target="tpu_custom_call" | custom-call | flops 2000000000 | bytes 60000000 | tf_op jit(solution)/shard_map/gap/pallas_call | solution.py:514
  55.6 1.0 %all-to-all-done.in_ref = f32[32,56,128]{2,1,0:T(8,128)S(1)} async-done(((f32[32,56,128]{2,1,0:T(8,128)}), f32[32,56,128]{2,1,0:T(8,128)S(1)}, u32[]{:S(2)}, u32[]{:S(2)}) %all-to-all-start) | async-done | bytes 917536 | tf_op jit(solution)/shard_map/all_to_all | solution.py:506
  56.6 1.8 %owner.1 = (f32[27,512]{1,0:T(8,128)}, f32[81,512]{1,0:T(8,128)}) custom-call(f32[32,56,128]{2,1,0:T(8,128)S(1)} %all-to-all-done.in_ref, bf16[81,32]{1,0:T(8,128)(2,1)S(1)} %copy-done), custom_call_target="tpu_custom_call" | custom-call | tf_op jit(solution)/shard_map/owner/pallas_call | solution.py:539
  (5 shorter events, 0.1 us)
Async XLA Ops:
  2.3 20.2 %collective-permute-start.2 = (f32[128,128]{1,0:T(8,128)}, f32[128,128]{1,0:T(8,128)S(1)}, u32[]{:S(2)}, u32[]{:S(2)}) collective-permute-start(f32[128,128]{1,0:T(8,128)} %get-tuple-element.22), channel_id=1, source_target_pairs={{24,0},{0,8},{8,16},{16,24},{25,1},{1,9},{9,17},{17,25},{26,2},{2,... | collective-permute-start | bytes 196616 | tf_op jit(solution)/shard_map/ppermute | solution.py:381
  5.3 17.2 %collective-permute-start.1 = (f32[128,128]{1,0:T(8,128)}, f32[128,128]{1,0:T(8,128)S(1)}, u32[]{:S(2)}, u32[]{:S(2)}) collective-permute-start(f32[128,128]{1,0:T(8,128)} %get-tuple-element.22), channel_id=1, source_target_pairs={{16,0},{24,8},{0,16},{8,24},{17,1},{25,9},{1,17},{9,25},{18,2},{26... | collective-permute-start | bytes 196616 | tf_op jit(solution)/shard_map/ppermute | solution.py:381
  7.9 14.6 %collective-permute-start = (f32[128,128]{1,0:T(8,128)}, f32[128,128]{1,0:T(8,128)S(1)}, u32[]{:S(2)}, u32[]{:S(2)}) collective-permute-start(f32[128,128]{1,0:T(8,128)} %get-tuple-element.22), channel_id=1, source_target_pairs={{8,0},{16,8},{24,16},{0,24},{9,1},{17,9},{25,17},{1,25},{10,2},{18... | collective-permute-start | bytes 196616 | tf_op jit(solution)/shard_map/ppermute | solution.py:381
  9.3 13.3 %copy-start.2 = (f32[128,128]{1,0:T(8,128)S(1)}, f32[128,128]{1,0:T(8,128)}, u32[]{:S(2)}) copy-start(f32[128,128]{1,0:T(8,128)} %get-tuple-element.22) | copy-start | bytes 196612
  22.6 10.7 %collective-permute-start.5 = (f32[512,128]{1,0:T(8,128)S(1)}, f32[512,128]{1,0:T(8,128)S(1)}, u32[]{:S(2)}, u32[]{:S(2)}) collective-permute-start(f32[512,128]{1,0:T(8,128)S(1)} %pad_maximum_fusion), channel_id=1, source_target_pairs={{6,0},{7,1},{4,2},{5,3},{2,4},{3,5},{0,6},{1,7},{14,8},{15,9},{12,... | collective-permute-start | bytes 786440 | tf_op jit(solution)/shard_map/ppermute | solution.py:389
  25.1 11.4 %collective-permute-start.4 = (f32[512,128]{1,0:T(8,128)S(1)}, f32[512,128]{1,0:T(8,128)S(1)}, u32[]{:S(2)}, u32[]{:S(2)}) collective-permute-start(f32[512,128]{1,0:T(8,128)S(1)} %pad_maximum_fusion), channel_id=1, source_target_pairs={{4,0},{5,1},{6,2},{7,3},{0,4},{1,5},{2,6},{3,7},{12,8},{13,9},{14,... | collective-permute-start | bytes 786440 | tf_op jit(solution)/shard_map/ppermute | solution.py:389
  25.6 11.8 %collective-permute-start.3 = (f32[512,128]{1,0:T(8,128)S(1)}, f32[512,128]{1,0:T(8,128)S(1)}, u32[]{:S(2)}, u32[]{:S(2)}) collective-permute-start(f32[512,128]{1,0:T(8,128)S(1)} %pad_maximum_fusion), channel_id=1, source_target_pairs={{2,0},{3,1},{0,2},{1,3},{6,4},{7,5},{4,6},{5,7},{10,8},{11,9},{8,1... | collective-permute-start | bytes 786440 | tf_op jit(solution)/shard_map/ppermute | solution.py:389
  30.2 10.1 %copy-start = (bf16[81,32]{1,0:T(8,128)(2,1)S(1)}, bf16[81,32]{1,0:T(8,128)(2,1)}, u32[]{:S(2)}) copy-start(bf16[81,32]{1,0:T(8,128)(2,1)} %constant.5.clone.expand_ref) | copy-start | bytes 15556
  30.2 10.1 %copy-start.1 = (s32[1,2048]{1,0:T(1,128)S(1)}, s32[1,2048]{1,0:T(1,128)}, u32[]{:S(2)}) copy-start(s32[1,2048]{1,0:T(1,128)} %get-tuple-element.27.row_ref) | copy-start | bytes 24580
  30.2 26.4 %all-to-all-start = ((f32[32,56,128]{2,1,0:T(8,128)}), f32[32,56,128]{2,1,0:T(8,128)S(1)}, u32[]{:S(2)}, u32[]{:S(2)}) async-start(f32[32,56,128]{2,1,0:T(8,128)} %slots.1), calls=%async_computation | async-start | bytes 1835008 | tf_op jit(solution)/shard_map/all_to_all | solution.py:506
  37.6 2.7 %collective-permute-start.6 = (f32[2048,128]{1,0:T(8,128)S(1)}, f32[2048,128]{1,0:T(8,128)S(1)}, u32[]{:S(2)}, u32[]{:S(2)}) collective-permute-start(f32[2048,128]{1,0:T(8,128)S(1)} %constant_dynamic-update-slice_fusion.near_ref), channel_id=1, source_target_pairs={{1,0},{0,1},{3,2},{2,3},{5,4},{4,5},{7,6},{6,7},{9,8},{8,9},{11,10... | collective-permute-start | bytes 3145736 | tf_op jit(solution)/shard_map/ppermute | solution.py:394
